TPU v7x, 256 devices: a whole 4x4x8 slice. The times are simulated.
256 devices in a mesh: seq: 64 (over z_lo, x, y), batch: 4 (over z_hi, core).
Axes of the slice: x: 4, y: 4, z: 8 (z_hi: 2, z_lo: 4; z = z_hi * 4 + z_lo), core: 2. Of those that a mesh axis runs over, the one named last changes fastest.
Arguments:
- inputs: bfloat16 [4, 16384, 2048], P('batch', 'seq'), may hold values from -106.50967 to 106.50967
- output_grad: bfloat16 [4, 16384, 2048], P('batch', 'seq'), may hold values from -6 to 6
- norm_gain: float32 [2048], replicated, may hold values from 0.1 to 1.9
- gate_bias: float32 [2048], P('seq'), as said below
- state_in: float32 [4, 2048], P('batch', 'seq'), may hold values from -6 to 6
- w_gate: bfloat16 [2048, 2048], P('seq'), may hold values from -0.44194174 to 0.44194174
- w_cand: bfloat16 [2048, 2048], P('seq'), may hold values from -0.125 to 0.125
- w_out: bfloat16 [2048, 2048], P('seq'), may hold values from -0.125 to 0.125
Outputs:
- layer_out: bfloat16 [4, 16384, 2048], P('batch', 'seq')
- input_grad: bfloat16 [4, 16384, 2048], P('batch', 'seq')
- state_grad: float32 [4, 2048], P('batch', 'seq')
- bias_grad: float32 [2048], P('seq')
Inputs may be any that keep to these rules, and one draw needn't show every extreme that they name: `gate_bias`: every value is at least -ln(16384) - 1.5.
All inputs are finite; a program needn't handle non-finite values.
Results may differ from a plain program's by a relative error of at most 0.013.
Values may be sent and summed in bfloat16 or wider, within the bound.
A program may use at most 128 MiB of HBM per device.

v0:
```python
import jax
import jax.numpy as jnp
from jax import lax
from jax.sharding import PartitionSpec as P

EPSILON = 1e-06


def shifted(values, axis, offset, fill, reverse):
    length = values.shape[axis]
    pad_shape = list(values.shape)
    pad_shape[axis] = offset
    padding = jnp.full(tuple(pad_shape), fill, values.dtype)
    if reverse:
        kept = lax.slice_in_dim(values, offset, length, 1, axis)
        return jnp.concatenate([kept, padding], axis=axis)
    kept = lax.slice_in_dim(values, 0, length - offset, 1, axis)
    return jnp.concatenate([padding, kept], axis=axis)


def shift_scan(keep, drive, axis, reverse):
    length = keep.shape[axis]
    offset = 1
    while offset < length:
        keep_far = shifted(keep, axis, offset, 1.0, reverse)
        drive_far = shifted(drive, axis, offset, 0.0, reverse)
        drive = keep * drive_far + drive
        keep = keep * keep_far
        offset = offset * 2
    return (keep, drive)


def on_device(inputs, output_grad, norm_gain, gate_bias, state_in, w_gate, w_cand, w_out):
    token_rows = inputs[0]
    grad_rows = output_grad[0]
    gate_full, cand_full, out_full = (
        lax.all_gather(w_gate, "seq", axis=0, tiled=True),
        lax.all_gather(w_cand, "seq", axis=0, tiled=True),
        lax.all_gather(w_out, "seq", axis=0, tiled=True),
    )
    residual = token_rows.astype(jnp.float32)
    mean_square = jnp.mean(residual * residual, axis=-1, keepdims=True)
    inverse_rms = lax.rsqrt(mean_square + EPSILON)
    unit_rows = residual * inverse_rms
    normed = (unit_rows * norm_gain).astype(jnp.bfloat16)
    hidden_dim = 0
    contract_model = (((0,), (1,)), ((), ()))
    gate_pre = lax.dot_general(
        gate_full, normed, contract_model, preferred_element_type=jnp.float32
    ).astype(jnp.bfloat16)
    cand_pre = lax.dot_general(
        cand_full, normed, contract_model, preferred_element_type=jnp.float32
    ).astype(jnp.bfloat16)
    back_grads = lax.dot_general(
        out_full, grad_rows, (((1,), (1,)), ((), ())), preferred_element_type=jnp.float32
    ).astype(jnp.bfloat16)
    gate_slab, cand_slab = (
        lax.all_to_all(gate_pre, "seq", split_axis=0, concat_axis=1, tiled=True),
        lax.all_to_all(cand_pre, "seq", split_axis=0, concat_axis=1, tiled=True),
    )
    gate_input = gate_slab.astype(jnp.float32) + gate_bias[:, None]
    update = jax.nn.sigmoid(gate_input)
    retain = jax.nn.sigmoid(-gate_input)
    candidate = cand_slab.astype(jnp.float32)
    initial = state_in[0]
    drive_term = (update * candidate).at[:, 0].add(retain[:, 0] * initial)
    reached, states = shift_scan(retain, drive_term, 1, False)
    state_tok = lax.all_to_all(
        states.astype(jnp.bfloat16), "seq", split_axis=1, concat_axis=0, tiled=True
    )
    back_slab = lax.all_to_all(back_grads, "seq", split_axis=0, concat_axis=1, tiled=True)
    next_retain = jnp.concatenate(
        [retain[:, 1:], jnp.zeros((retain.shape[0], 1), jnp.float32)], axis=1
    )
    tail_keep, carried = shift_scan(next_retain, back_slab.astype(jnp.float32), 1, True)
    state_grad = retain[:, 0] * carried[:, 0]
    earlier_states = jnp.concatenate([initial[:, None], states[:, :-1]], axis=1)
    gate_grad = carried * (candidate - earlier_states) * update * retain
    cand_grad = carried * update
    bias_part = jnp.sum(gate_grad, axis=1)
    gate_tok, cand_tok = (
        lax.all_to_all(
            gate_grad.astype(jnp.bfloat16), "seq", split_axis=1, concat_axis=0, tiled=True
        ),
        lax.all_to_all(
            cand_grad.astype(jnp.bfloat16), "seq", split_axis=1, concat_axis=0, tiled=True
        ),
    )
    contract_hidden = (((hidden_dim,), (0,)), ((), ()))
    layer_rows = (
        residual
        + lax.dot_general(state_tok, out_full, contract_hidden, preferred_element_type=jnp.float32)
    ).astype(jnp.bfloat16)
    contract_back = (((hidden_dim,), (1,)), ((), ()))
    normed_grad = lax.dot_general(
        gate_tok, gate_full, contract_back, preferred_element_type=jnp.float32
    )
    normed_grad = normed_grad + lax.dot_general(
        cand_tok, cand_full, contract_back, preferred_element_type=jnp.float32
    )
    unit_grad = normed_grad * norm_gain
    input_rows = inverse_rms * (
        unit_grad - unit_rows * jnp.mean(unit_grad * unit_rows, axis=-1, keepdims=True)
    )
    token_grad = (grad_rows.astype(jnp.float32) + input_rows).astype(jnp.bfloat16)
    bias_grad = lax.psum(bias_part, "batch")
    return (layer_rows[None], token_grad[None], state_grad[None], bias_grad)


def solution(mesh):
    return jax.shard_map(
        on_device,
        mesh=mesh,
        in_specs=(
            P("batch", "seq", None),
            P("batch", "seq", None),
            P(),
            P("seq"),
            P("batch", "seq"),
            P("seq", None),
            P("seq", None),
            P("seq", None),
        ),
        out_specs=(P("batch", "seq", None), P("batch", "seq", None), P("batch", "seq"), P("seq")),
        check_vma=False,
    )
```

profile of v0, /device:TPU:1, one launch (start us, length us, event | category | flops | bytes accessed | tf_op | source)
XLA Modules:
  0.0 1304.9 jit_solution(2977227251477616313)
XLA Ops:
  7.2 0.7 all-gather.6.cloned.1.call-update
  7.9 0.7 all-gather.4.cloned.1.call-update
  8.7 0.7 all-gather.8.cloned.1.call-update
  9.4 1.5 fusion.14
  10.9 319.6 %all-gather.6.cloned.1.call-done = bf16[2048,2048]{1,0:T(8,128)(2,1)} async-done(((bf16[32,2048]{1,0:T(8,128)(2,1)}), bf16[2048,2048]{1,0:T(8,128)(2,1)}) %all-gather.6.cloned.1.call-update) | async-done | bytes 8388624 | tf_op jit(solution)/shard_map/all_gather | solution.py:38
  330.5 6.1 fusion.6
  336.6 1.3 copy.33
  338.0 8.1 all-to-all-start.1
  346.0 345.6 %all-gather.4.cloned.1.call-done = bf16[2048,2048]{1,0:T(8,128)(2,1)} async-done(((bf16[32,2048]{1,0:T(8,128)(2,1)}), bf16[2048,2048]{1,0:T(8,128)(2,1)}) %all-gather.4.cloned.1.call-update) | async-done | bytes 8388624 | tf_op jit(solution)/shard_map/all_gather | solution.py:37
  691.6 6.7 fusion.5
  698.3 2.3 copy.31
  700.7 8.3 all-to-all-start
  709.0 345.7 %all-gather.8.cloned.1.call-done = bf16[2048,2048]{1,0:T(8,128)(2,1)} async-done(((bf16[32,2048]{1,0:T(8,128)(2,1)}), bf16[2048,2048]{1,0:T(8,128)(2,1)}) %all-gather.8.cloned.1.call-update) | async-done | bytes 8388624 | tf_op jit(solution)/shard_map/all_gather | solution.py:39
  1054.6 6.7 convolution_convert_fusion
  1061.4 8.0 all-to-all-start.3
  1069.6 0.6 compare_reduce_fusion
  1070.5 1.6 copy.45
  1072.3 1.5 copy.44
  1073.9 14.3 %all-to-all-done.3 = bf16[64,32,256]{2,1,0:T(8,128)(2,1)} async-done(((bf16[64,32,256]{2,1,0:T(8,128)(2,1)}), bf16[64,32,256]{2,1,0:T(8,128)(2,1)}, u32[]{:S(2)}, u32[]{:S(2)}) %all-to-all-start.3) | async-done | bytes 1048608 | tf_op jit(solution)/shard_map/all_to_all | solution.py:71
  1088.1 1.5 convert_bitcast_fusion
  1089.8 2.0 slice.294
  1091.9 1.0 copy-done.2
  1092.9 0.6 copy-done.8
  1093.5 1.2 add_divide_fusion.1
  1094.7 2.6 fusion.27
  1097.3 0.7 add_select_fusion
  1098.0 1.3 scatter-add.4
  1099.3 4.3 multiply_add_fusion.27
  1104.2 1.0 copy-done.6
  1105.2 0.6 copy-done.14
  1106.3 2.5 slice_multiply_fusion
  1109.8 2.1 slice.296
  1111.9 10.3 multiply_add_fusion.11
  1122.1 4.6 multiply_add_fusion.25
  1126.8 1.1 multiply_add_fusion.24
  1127.9 1.1 multiply_add_fusion.23
  1129.1 1.1 multiply_add_fusion.22
  1130.2 1.1 multiply_add_fusion.21
  1131.5 9.4 multiply_add_fusion.20
  1144.5 1.5 copy-done.10
  1146.6 1.0 copy-done.11
  1148.6 0.6 slice.298
  1149.2 0.6 slice.284
  1150.8 0.6 slice.285
  1152.5 0.6 slice.286
  1155.0 0.6 multiply_add_fusion.5
  1158.9 1.2 copy-done.3
  1160.1 0.6 copy-done.9
  1160.7 2.9 fusion.24
  1163.6 1.1 copy.51
  1164.7 5.5 all-to-all-start.4
  1170.2 2.8 multiply_convert_fusion
  1173.1 1.1 copy.50
  1174.2 13.8 %all-to-all-done.4 = bf16[32,64,256]{2,0,1:T(8,128)(2,1)} async-done(((bf16[32,64,256]{2,0,1:T(8,128)(2,1)}), bf16[32,64,256]{2,0,1:T(8,128)(2,1)}, u32[]{:S(2)}, u32[]{:S(2)}) %all-to-all-start.4) | async-done | bytes 1048608 | tf_op jit(solution)/shard_map/all_to_all | solution.py:82
  1188.0 5.5 all-to-all-start.5
  1193.6 1.1 copy.52
  1194.7 58.4 %psum.7 = f32[32]{0:T(128)} all-reduce(f32[32]{0:T(128)S(1)} %get-tuple-element.16), channel_id=1, replica_groups=mesh['seq'=64,'batch'=4] {'batch'}, use_global_device_ids=true, to_apply=%region_4.0 | all-reduce | flops 32 | bytes 256 | tf_op jit(solution)/shard_map/psum | solution.py:106
  1253.1 1.3 fusion.22
  1254.4 10.6 all-to-all-start.2
  1265.1 6.2 fusion.28
  1271.3 6.5 fusion.9
  1277.8 1.6 fusion.18
  1279.4 11.8 all-to-all-done.2
  1291.3 6.7 fusion.7
  (104 shorter events, 15.4 us)
Async XLA Ops:
  7.2 323.3 %all-gather.6.cloned.1.call-start = ((), (), s32[]{:S(2)}) async-start(), calls=%async_computation.7 | async-start | bytes 8519680 | tf_op jit(solution)/shard_map/all_gather | solution.py:38
  7.9 683.7 %all-gather.4.cloned.1.call-start = ((), (), s32[]{:S(2)}) async-start(), calls=%async_computation.6 | async-start | bytes 8519680 | tf_op jit(solution)/shard_map/all_gather | solution.py:37
  8.6 1046.0 %all-gather.8.cloned.1.call-start = ((), (), s32[]{:S(2)}) async-start(), calls=%async_computation.8 | async-start | bytes 8519680 | tf_op jit(solution)/shard_map/all_gather | solution.py:39
  10.9 680.7 %copy-start.20 = (f32[256]{0:T(256)}, f32[256]{0:T(256)S(1)}, u32[]{:S(2)}) copy-start(f32[256]{0:T(256)S(1)} %add_rsqrt_fusion) | copy-start | bytes 3076
  336.6 355.0 %copy-start.12 = (bf16[1,256,2048]{2,1,0:T(8,128)(2,1)S(1)}, bf16[1,256,2048]{2,1,0:T(8,128)(2,1)}, u32[]{:S(2)}) copy-start(bf16[1,256,2048]{2,1,0:T(8,128)(2,1)} %param.10) | copy-start | bytes 3145732
  336.6 355.0 %copy-start.23 = (f32[2048]{0:T(1024)S(1)}, f32[2048]{0:T(1024)}, u32[]{:S(2)}) copy-start(f32[2048]{0:T(1024)} %param.12) | copy-start | bytes 24580
  338.0 362.7 %all-to-all-start.1 = ((bf16[64,32,256]{2,1,0:T(8,128)(2,1)}), bf16[64,32,256]{2,1,0:T(8,128)(2,1)S(1)}, u32[]{:S(2)}, u32[]{:S(2)}) async-start(bf16[64,32,256]{2,1,0:T(8,128)(2,1)} %bitcast.6), calls=%async_computation.1 | async-start | bytes 2097152 | tf_op jit(solution)/shard_map/all_to_all | solution.py:59
  698.3 356.3 %copy-start.17 = (bf16[1,256,2048]{2,1,0:T(8,128)(2,1)S(1)}, bf16[1,256,2048]{2,1,0:T(8,128)(2,1)}, u32[]{:S(2)}) copy-start(bf16[1,256,2048]{2,1,0:T(8,128)(2,1)} %param.11) | copy-start | bytes 3145732
  700.7 360.7 %all-to-all-start = ((bf16[64,32,256]{2,1,0:T(8,128)(2,1)}), bf16[64,32,256]{2,1,0:T(8,128)(2,1)S(1)}, u32[]{:S(2)}, u32[]{:S(2)}) async-start(bf16[64,32,256]{2,1,0:T(8,128)(2,1)} %bitcast.3), calls=%async_computation | async-start | bytes 2097152 | tf_op jit(solution)/shard_map/all_to_all | solution.py:58
  1061.4 8.1 copy-start.22
  1061.4 8.2 copy-start.15
  1061.4 26.7 %all-to-all-start.3 = ((bf16[64,32,256]{2,1,0:T(8,128)(2,1)}), bf16[64,32,256]{2,1,0:T(8,128)(2,1)}, u32[]{:S(2)}, u32[]{:S(2)}) async-start(bf16[64,32,256]{2,1,0:T(8,128)(2,1)} %bitcast.110), calls=%async_computation.3 | async-start | bytes 2097152 | tf_op jit(solution)/shard_map/all_to_all | solution.py:71
  1070.4 1.6 copy-start.16
  1089.8 2.1 copy-start.5
  1089.8 3.1 copy-start.2
  1089.8 3.7 copy-start.8
  1089.8 3.7 copy-start.19
  1094.7 2.6 copy-start.4
  1099.3 4.3 copy-start
  1103.6 1.6 copy-start.6
  1103.6 2.2 copy-start.14
  1105.8 3.5 copy-start.1
  1109.8 2.1 copy-start.7
  1144.4 1.6 copy-start.10
  1146.0 1.6 copy-start.11
  1158.5 1.6 copy-start.3
  1158.5 2.2 copy-start.9
  1164.7 23.3 %all-to-all-start.4 = ((bf16[32,64,256]{2,0,1:T(8,128)(2,1)}), bf16[32,64,256]{2,0,1:T(8,128)(2,1)}, u32[]{:S(2)}, u32[]{:S(2)}) async-start(bf16[32,64,256]{2,0,1:T(8,128)(2,1)} %bitcast.107), calls=%async_computation.4 | async-start | bytes 2097152 | tf_op jit(solution)/shard_map/all_to_all | solution.py:82
  1188.0 66.4 %all-to-all-start.5 = ((bf16[32,64,256]{2,0,1:T(8,128)(2,1)}), bf16[32,64,256]{2,0,1:T(8,128)(2,1)}, u32[]{:S(2)}, u32[]{:S(2)}) async-start(bf16[32,64,256]{2,0,1:T(8,128)(2,1)} %bitcast.106), calls=%async_computation.5 | async-start | bytes 2097152 | tf_op jit(solution)/shard_map/all_to_all | solution.py:85
  1254.4 36.8 %all-to-all-start.2 = ((bf16[32,64,256]{2,0,1:T(8,128)(2,1)}), bf16[32,64,256]{2,0,1:T(8,128)(2,1)S(1)}, u32[]{:S(2)}, u32[]{:S(2)}) async-start(bf16[32,64,256]{2,0,1:T(8,128)(2,1)} %bitcast.105), calls=%async_computation.2 | async-start | bytes 2097152 | tf_op jit(solution)/shard_map/all_to_all | solution.py:68
  1265.0 6.2 copy-start.13
  1265.0 6.2 copy-start.21
  1265.1 6.2 copy-start.24
  1271.3 6.5 copy-start.18
Sparse Core Ops, SparseCore 0:
  9.8 320.7 all-gather.5
  332.3 359.2 all-gather.3
  693.4 361.2 all-gather.7
where the time goes:
time: 1310 us; the launch traced here: 1300 us
  waiting for transfers between devices  1050 us (80%)
  blocking collectives  58.4 us (4%)
  other arithmetic  57.8 us (4%)
  starting transfers between devices  46.1 us (4%)
  matrix products  39 us (3%)
  local copies, waits for them, and re-layouts  36 us (3%)
  between operations  14.9 us (1%)
    all_gather x1, waiting for transfers between devices, on_device(): lax.all_gather(w_out, 'seq', axis=0, tiled=True)  346 us
    all_gather x1, waiting for transfers between devices, on_device(): lax.all_gather(w_gate, 'seq', axis=0, tiled=True)  346 us
    all_gather x1, waiting for transfers between devices, on_device(): lax.all_gather(w_cand, 'seq', axis=0, tiled=True)  320 us
    psum x1, blocking collectives, on_device(): bias_grad = lax.psum(bias_part, 'batch')  58.4 us
    add x25, other arithmetic, shift_scan(): drive = keep * drive_far + drive  40.3 us
  transfers between devices with their start and end apart: 9, of which 6 were waited for; matrix products, arithmetic and copies ran while one was open for 4% of the time, Pallas kernels for 0%

commit v1 on v0

v1 whole, which is shorter than its diff:
```python
import functools
import jax
import jax.numpy as jnp
from jax import lax
from jax.sharding import PartitionSpec as P
from jax.experimental import pallas as pl
from jax.experimental.pallas import tpu as pltpu

EPSILON = 1e-06
MESH = pl.DeviceIdType.MESH
ORDERS = ("yxz", "zyx", "xzy")
AXIS_DIM = {"z": 0, "x": 1, "y": 2}
CHUNKS = 2


class Place:
    def __init__(self):
        seq = lax.axis_index("seq")
        batch = lax.axis_index("batch")
        self.seq, self.batch = seq, batch
        self.at = {"z": seq // 16, "x": lax.rem(seq // 4, 4), "y": lax.rem(seq, 4)}
        self.z_hi = batch // 2
        self.core = lax.rem(batch, 2)

    def device(self, z, x, y, z_hi, core):
        return (z * 16 + x * 4 + y, z_hi * 2 + core)

    def ring(self, axis, step):
        z, x, y = self.at["z"], self.at["x"], self.at["y"]
        if axis == "x":
            return self.device(z, lax.rem(x + 4 + step, 4), y, self.z_hi, self.core)
        if axis == "y":
            return self.device(z, x, lax.rem(y + 4 + step, 4), self.z_hi, self.core)
        full = lax.rem(self.z_hi * 4 + z + 8 + step, 8)
        return self.device(lax.rem(full, 4), x, y, full // 4, self.core)

    def sibling(self):
        return (self.seq, self.z_hi * 2 + 1 - self.core)


def gather_kernel(
    gate_ref, cand_ref, out_ref, full_ref, weights, own_sem, send_sem, recv_sem, sib_send, sib_recv, put_sem
):
    place = Place()
    core = place.core
    shards = (out_ref, gate_ref, cand_ref)
    own = []
    for w in range(3):
        for half in range(2):
            copy = pltpu.make_async_copy(
                shards[w].at[pl.ds(16 * half, 16), :],
                weights.at[w, place.at["z"], place.at["x"], place.at["y"], half],
                own_sem.at[w, half],
            )
            copy.start()
            own.append(copy)
    barrier = pltpu.get_barrier_semaphore()
    peers = [place.ring(a, d) for a in "xyz" for d in (1, -1)] + [place.sibling()]
    for peer in peers:
        pl.semaphore_signal(barrier, inc=1, device_id=peer, device_id_type=MESH)
    pl.semaphore_wait(barrier, len(peers))
    for copy in own:
        copy.wait()

    def slab(w, phase, step, which, cols):
        order = ORDERS[w]
        index = [None, None, None]
        for position, axis in enumerate(order):
            own_at = place.at[axis]
            if position < phase:
                index[AXIS_DIM[axis]] = slice(None)
            elif position == phase:
                index[AXIS_DIM[axis]] = lax.rem(own_at + 4 + step, 4)
            else:
                index[AXIS_DIM[axis]] = own_at
        return weights.at[w, index[0], index[1], index[2], which, :, pl.ds(cols[0], cols[1])]

    def chunks(phase):
        n = CHUNKS if phase == 2 else 1
        return [(q, (2048 // n * q, 2048 // n)) for q in range(n)]

    def piece(w, phase, kind, cols, outgoing):
        right = kind % 2 == 0
        if kind < 2:
            span = cols
            step = 0 if outgoing else (-1 if right else 1)
        else:
            span = (cols[0], cols[1] // 2) if right else (cols[0] + cols[1] // 2, cols[1] // 2)
            step = (-1 if right else 1) if outgoing else 2
        return step, span

    def send(w, phase, kind, q, cols):
        step, span = piece(w, phase, kind, cols, True)
        ref = slab(w, phase, step, core, span)
        return pltpu.make_async_remote_copy(
            src_ref=ref, dst_ref=ref,
            send_sem=send_sem.at[w, phase, kind, q], recv_sem=recv_sem.at[w, phase, kind, q],
            device_id=place.ring(ORDERS[w][phase], 1 if kind % 2 == 0 else -1), device_id_type=MESH,
        )

    def arrival(w, phase, kind, q, cols):
        step, span = piece(w, phase, kind, cols, False)
        ref = slab(w, phase, step, core, span)
        return pltpu.make_async_remote_copy(
            src_ref=ref, dst_ref=ref,
            send_sem=send_sem.at[w, phase, kind, q], recv_sem=recv_sem.at[w, phase, kind, q],
            device_id=place.ring(ORDERS[w][phase], 1 if kind % 2 == 0 else -1), device_id_type=MESH,
        )

    def share(w, phase, kind, q, cols, mine):
        step, span = piece(w, phase, kind, cols, False)
        ref = slab(w, phase, step, core if mine else 1 - core, span)
        return pltpu.make_async_remote_copy(
            src_ref=ref, dst_ref=ref,
            send_sem=sib_send.at[w, phase, kind, q], recv_sem=sib_recv.at[w, phase, kind, q],
            device_id=place.sibling(), device_id_type=MESH,
        )

    for phase in range(3):
        for q, cols in chunks(phase):
            for w in range(3):
                for kind in (0, 1):
                    send(w, phase, kind, q, cols).start()
        for q, cols in chunks(phase):
            for w in range(3):
                for kind in (0, 1):
                    arrival(w, phase, kind, q, cols).wait_recv()
                    send(w, phase, kind + 2, q, cols).start()
                    share(w, phase, kind, q, cols, True).start()
        for q, cols in chunks(phase):
            for w in range(3):
                for kind in (2, 3):
                    arrival(w, phase, kind, q, cols).wait_recv()
                    share(w, phase, kind, q, cols, True).start()
    for phase in range(3):
        for q, cols in chunks(phase):
            for w in range(3):
                for kind in range(4):
                    share(w, phase, kind, q, cols, False).wait_recv()
                    share(w, phase, kind, q, cols, True).wait_send()
                    send(w, phase, kind, q, cols).wait_send()
    put = pltpu.make_async_copy(weights, full_ref, put_sem)
    put.start()
    put.wait()


def gather_weights(w_gate, w_cand, w_out):
    full = pl.pallas_call(
        gather_kernel,
        out_shape=jax.ShapeDtypeStruct((3, 4, 4, 4, 2, 16, 2048), jnp.bfloat16),
        in_specs=[pl.BlockSpec(memory_space=pltpu.VMEM)] * 3,
        out_specs=pl.BlockSpec(memory_space=pl.ANY),
        scratch_shapes=[
            pltpu.VMEM((3, 4, 4, 4, 2, 16, 2048), jnp.bfloat16),
            pltpu.SemaphoreType.DMA((3, 2)),
            pltpu.SemaphoreType.DMA((3, 3, 4, CHUNKS)),
            pltpu.SemaphoreType.DMA((3, 3, 4, CHUNKS)),
            pltpu.SemaphoreType.DMA((3, 3, 4, CHUNKS)),
            pltpu.SemaphoreType.DMA((3, 3, 4, CHUNKS)),
            pltpu.SemaphoreType.DMA,
        ],
        compiler_params=pltpu.CompilerParams(collective_id=0, has_side_effects=True, vmem_limit_bytes=60 * 1024 * 1024),
        name="weights",
    )(w_gate, w_cand, w_out)
    full = full.reshape(3, 2048, 2048)
    return full[1], full[2], full[0]


def shifted(values, axis, offset, fill, reverse):
    length = values.shape[axis]
    pad_shape = list(values.shape)
    pad_shape[axis] = offset
    padding = jnp.full(tuple(pad_shape), fill, values.dtype)
    if reverse:
        kept = lax.slice_in_dim(values, offset, length, 1, axis)
        return jnp.concatenate([kept, padding], axis=axis)
    kept = lax.slice_in_dim(values, 0, length - offset, 1, axis)
    return jnp.concatenate([padding, kept], axis=axis)


def shift_scan(keep, drive, axis, reverse):
    length = keep.shape[axis]
    offset = 1
    while offset < length:
        keep_far = shifted(keep, axis, offset, 1.0, reverse)
        drive_far = shifted(drive, axis, offset, 0.0, reverse)
        drive = keep * drive_far + drive
        keep = keep * keep_far
        offset = offset * 2
    return (keep, drive)


def on_device(inputs, output_grad, norm_gain, gate_bias, state_in, w_gate, w_cand, w_out):
    token_rows = inputs[0]
    grad_rows = output_grad[0]
    seq = lax.axis_index("seq")
    gate_full, cand_full, out_full = gather_weights(w_gate, w_cand, w_out)
    bias_full = lax.all_gather(gate_bias, "seq", axis=0, tiled=True)
    initial_full = lax.all_gather(state_in[0], "seq", axis=0, tiled=True)
    residual = token_rows.astype(jnp.float32)
    mean_square = jnp.mean(residual * residual, axis=-1, keepdims=True)
    inverse_rms = lax.rsqrt(mean_square + EPSILON)
    unit_rows = residual * inverse_rms
    normed = (unit_rows * norm_gain).astype(jnp.bfloat16)
    gate_pre = jnp.dot(normed, gate_full, preferred_element_type=jnp.float32).astype(jnp.bfloat16)
    cand_pre = jnp.dot(normed, cand_full, preferred_element_type=jnp.float32).astype(jnp.bfloat16)
    back = lax.dot_general(
        grad_rows, out_full, (((1,), (1,)), ((), ())), preferred_element_type=jnp.float32
    ).astype(jnp.bfloat16).astype(jnp.float32)
    gate_input = gate_pre.astype(jnp.float32) + bias_full
    update = jax.nn.sigmoid(gate_input)
    retain = jax.nn.sigmoid(-gate_input)
    candidate = cand_pre.astype(jnp.float32)
    reach, local_states = shift_scan(retain, update * candidate, 0, False)
    tail_reach, local_carry = shift_scan(retain, retain * back, 0, True)
    summary = jnp.stack([reach[-1], local_states[-1], local_carry[0]])
    every = lax.all_gather(summary, "seq", axis=0)
    keeps, ends, carries = every[:, 0], every[:, 1], every[:, 2]
    ends = ends.at[0].add(keeps[0] * initial_full)
    _, prefix = shift_scan(keeps, ends, 0, False)
    _, suffix = shift_scan(keeps, carries, 0, True)
    entering = jnp.where(seq == 0, initial_full, prefix[jnp.maximum(seq - 1, 0)])
    leaving = jnp.where(seq == 63, 0.0, suffix[jnp.minimum(seq + 1, 63)])
    state_grad = lax.dynamic_slice(suffix[0], (seq * 32,), (32,))
    states = local_states + reach * entering
    earlier = jnp.concatenate([entering[None], states[:-1]], axis=0)
    scaled = local_carry + tail_reach * leaving
    carried = back + jnp.concatenate([scaled[1:], leaving[None]], axis=0)
    gate_grad = carried * (candidate - earlier) * update * retain
    cand_grad = carried * update
    bias_part = jnp.sum(gate_grad, axis=0)
    layer_rows = (
        residual + jnp.dot(states.astype(jnp.bfloat16), out_full, preferred_element_type=jnp.float32)
    ).astype(jnp.bfloat16)
    back_dims = (((1,), (1,)), ((), ()))
    normed_grad = lax.dot_general(
        gate_grad.astype(jnp.bfloat16), gate_full, back_dims, preferred_element_type=jnp.float32
    ) + lax.dot_general(
        cand_grad.astype(jnp.bfloat16), cand_full, back_dims, preferred_element_type=jnp.float32
    )
    unit_grad = normed_grad * norm_gain
    input_rows = inverse_rms * (
        unit_grad - unit_rows * jnp.mean(unit_grad * unit_rows, axis=-1, keepdims=True)
    )
    token_grad = (grad_rows.astype(jnp.float32) + input_rows).astype(jnp.bfloat16)
    bias_grad = lax.psum(lax.psum_scatter(bias_part, "seq", scatter_dimension=0, tiled=True), "batch")
    return (layer_rows[None], token_grad[None], state_grad[None], bias_grad)


def solution(mesh):
    return jax.shard_map(
        on_device,
        mesh=mesh,
        in_specs=(
            P("batch", "seq", None),
            P("batch", "seq", None),
            P(),
            P("seq"),
            P("batch", "seq"),
            P("seq", None),
            P("seq", None),
            P("seq", None),
        ),
        out_specs=(P("batch", "seq", None), P("batch", "seq", None), P("batch", "seq"), P("seq")),
        check_vma=False,
    )
```

time: 1310 us -> 1120 us (0.85)
  waiting for transfers between devices: 1050 us -> 350 us
  blocking collectives: 58.4 us -> 556 us
  Pallas kernels: 0 us -> 77.9 us
  starting transfers between devices: 46.1 us -> 0.04 us
  local copies, waits for them, and re-layouts: 36 us -> 56.6 us
  other arithmetic: 57.8 us -> 40.1 us
  matrix products: 39 us -> 24 us
    all_gather x3 -> x1, waiting for transfers between devices: 1010 us -> 350 us  [on_device(): every = lax.all_gather(summary, 'seq', axis=0)]
    unnamed x0 -> x2, blocking collectives: none -> 470 us
    pallas_call x0 -> x1, Pallas kernels: none -> 77.9 us  [gather_weights(): pl.pallas_call(gather_kernel, out_shape=jax.ShapeDtypeStruct((3, 4, 4, 4,...]
    all_to_all x6 -> x0, starting transfers between devices: 46 us -> none  [the longest x1 10.6 us: on_device(): lax.all_to_all(states.astype(jnp.bfloat16), 'seq', split_axis=1, concat_a...]
    all_to_all x6 -> x0, waiting for transfers between devices: 39.9 us -> none  [the longest x1 14.3 us: on_device(): lax.all_to_all(back_grads, 'seq', split_axis=0, concat_axis=1, tiled=True)]
    psum x1, blocking collectives: 58.4 us -> 85.9 us  [on_device(): lax.psum(lax.psum_scatter(bias_part, 'seq', scatter_dimension=0, tiled=Tr...]
    slice x1 -> x6, local copies, waits for them, and re-layouts: 2.62 us -> 22 us  [the longest x1 16.9 us: gather_weights(): return (full[1], full[2], full[0])]
    dot_general x6, matrix products: 39 us -> 24 us  [the longest x1 5.9 us: on_device(): jnp.dot(normed, cand_full, preferred_element_type=jnp.float32)]
  transfers between devices with their start and end apart: 9 -> 1, of which waited for: 6 -> 1; matrix products, arithmetic and copies ran while one was open for 4% -> 0% of each run, Pallas kernels for 0% -> 0%
where the time goes in v1:
time: 1120 us
  blocking collectives  556 us (50%)
  waiting for transfers between devices  350 us (31%)
  Pallas kernels  77.9 us (7%)
  local copies, waits for them, and re-layouts  56.6 us (5%)
  other arithmetic  40.1 us (4%)
  matrix products  24 us (2%)
  between operations  16.5 us (1%)
    unnamed x2, blocking collectives  470 us
    all_gather x1, waiting for transfers between devices, on_device(): every = lax.all_gather(summary, 'seq', axis=0)  350 us
    psum x1, blocking collectives, on_device(): lax.psum(lax.psum_scatter(bias_part, 'seq', scatter_dimension=0, tiled=Tr...  85.9 us
    pallas_call x1, Pallas kernels, gather_weights(): pl.pallas_call(gather_kernel, out_shape=jax.ShapeDtypeStruct((3, 4, 4, 4,...  77.9 us
    add x24, other arithmetic, shift_scan(): drive = keep * drive_far + drive  33.3 us
  transfers between devices with their start and end apart: 1, of which 1 were waited for; matrix products, arithmetic and copies ran while one was open for 0% of the time, Pallas kernels for 0%

profile of v1, /device:TPU:1, one launch (start us, length us, event | category | flops | bytes accessed | tf_op | source)
XLA Modules:
  0.0 1120.4 jit_solution(1498064525150850209)
XLA Ops:
  7.2 77.9 %weights.1 = bf16[3,4,4,4,2,16,2048]{6,5,4,3,2,1,0:T(8,128)(2,1)} custom-call(bf16[32,2048]{1,0:T(8,128)(2,1)} %gate_ref.1, bf16[32,2048]{1,0:T(8,128)(2,1)} %cand_ref.1, bf16[32,2048]{1,0:T(8,128)(2,1)} %out_ref.1), custom_call_target="tpu_custom_call" | custom-call | tf_op jit(solution)/shard_map/weights/pallas_call | solution.py:148
  85.2 16.9 %fusion.39 = (bf16[1,4,4,4,2,16,2048]{6,5,4,3,2,1,0:T(8,128)(2,1)}, bf16[1,4,4,4,2,16,2048]{6,5,4,3,2,1,0:T(8,128)(2,1)}, bf16[1,4,4,4,2,16,2048]{6,5,4,3,2,1,0:T(8,128)(2,1)}) fusion(bf16[3,4,4,4,2,16,2048]{6,5,4,3,2,1,0:T(8,128)(2,1)} %weights.1), kind=kLoop, calls=%fused_computation.117 | loop fusion | bytes 50331648 | tf_op jit(solution)/shard_map/slice | solution.py:166
  102.1 0.3 fusion.20
  102.4 0.6 fusion.45
  103.8 0.3 dynamic-update-slice.3
  104.1 308.7 %all-reduce.57 = (f32[2048]{0:T(1024)S(1)}, f32[2048]{0:T(1024)S(1)}) all-reduce(f32[2048]{0:T(1024)S(1)} %dynamic-update-slice.3, f32[2048]{0:T(1024)S(1)} %bitcast_dynamic-update-slice_fusion), channel_id=1, replica_groups=mesh['seq'=64,'batch'=4] {'seq'}, use_global_device_ids=true, to_apply=%add.54 | all-reduce | flops 4096 | bytes 32768
  412.8 5.9 convolution_convert_fusion.1
  418.8 2.4 fusion.8
  421.2 2.1 copy-done.13
  423.5 2.9 fusion.36
  426.7 1.1 copy-done.14
  427.8 2.7 multiply_add_fusion.8
  430.5 2.5 fusion.43
  432.9 1.5 slice.333
  434.5 7.7 multiply_add_fusion.7
  442.1 1.8 slice.326
  444.1 0.7 copy-done
  444.7 1.7 slice.334
  446.4 8.9 multiply_add_fusion.6
  455.3 0.3 slice.327
  455.6 1.3 copy-done.5
  457.1 1.2 multiply_add_fusion.5
  458.7 1.1 multiply_add_fusion.4
  460.3 1.1 multiply_add_fusion.3
  461.7 0.9 multiply_add_fusion.2
  462.9 0.7 multiply_add_fusion.1
  463.6 0.9 copy-done.4
  464.7 0.2 copy-done.10
  465.0 1.2 multiply_add_fusion.13
  466.6 1.1 multiply_add_fusion.12
  468.2 1.1 multiply_add_fusion.11
  469.6 1.0 multiply_add_fusion.10
  470.9 0.9 multiply_add_fusion.9
  472.2 1.5 copy-done.6
  473.7 0.3 copy-done.8
  474.0 0.6 maximum_bitcast_fusion
  474.7 1.1 slice.356
  476.4 349.6 %all-gather.5.cloned.1.call-done = f32[64,3,2048]{2,1,0:T(4,128)} async-done(((f32[1,3,2048]{2,1,0:T(4,128)}), f32[64,3,2048]{2,1,0:T(4,128)}) %all-gather.5.cloned.1.call-update) | async-done | bytes 1572880 | tf_op jit(solution)/shard_map/all_gather | solution.py:217
  825.9 5.0 fusion.41
  831.2 1.7 fusion.40
  833.1 0.4 fusion.30
  833.5 0.9 slice.364
  834.4 1.0 copy.43
  835.6 1.8 multiply_add_fusion.21
  838.1 1.1 copy-done.22
  839.3 0.4 multiply_add_fusion.25
  840.4 1.5 copy-done.7
  841.9 0.6 copy-done.9
  842.5 0.3 multiply_add_fusion
  842.9 0.3 slice-done.5
  843.2 0.7 copy-done.20
  843.9 3.4 fusion.11
  847.4 1.5 copy-done.11
  848.9 0.6 slice_add_fusion
  849.4 1.0 copy-done.3
  850.4 0.6 copy-done.15
  851.1 0.3 copy-done.26
  851.3 1.6 fusion.37
  853.0 3.7 fusion.27
  856.8 5.7 fusion.12
  862.5 161.1 %all-reduce.56 = f32[2048]{0:T(1024)S(1)} all-reduce(f32[2048]{0:T(1024)S(1)} %get-tuple-element.18), channel_id=4, replica_groups=mesh['seq'=64,'batch'=4] {'seq'}, use_global_device_ids=true, to_apply=%region_3.4.clone | all-reduce | flops 2048 | bytes 16384
  1023.6 85.9 %psum.7 = f32[32]{0:T(128)} all-reduce(f32[32]{0:T(128)S(1)} %dynamic-slice.13), channel_id=1, replica_groups=mesh['seq'=64,'batch'=4] {'batch'}, use_global_device_ids=true, to_apply=%region_4.5 | all-reduce | flops 32 | bytes 256 | tf_op jit(solution)/shard_map/psum | solution.py:246
  1109.6 3.2 fusion.25
  1112.8 0.6 constant_dynamic-slice_fusion
  (121 shorter events, 6.4 us)
Async XLA Ops:
  7.2 818.8 %all-gather.5.cloned.1.call-start = ((), (), s32[]{:S(2)}) async-start(), calls=%async_computation | async-start | bytes 2129920 | tf_op jit(solution)/shard_map/all_gather | solution.py:217
  85.1 17.0 %copy-start.19 = (bf16[1,256,2048]{2,1,0:T(8,128)(2,1)S(1)}, bf16[1,256,2048]{2,1,0:T(8,128)(2,1)}, u32[]{:S(2)}) copy-start(bf16[1,256,2048]{2,1,0:T(8,128)(2,1)} %param.10) | copy-start | bytes 3145732
  85.1 17.3 %copy-start.27 = (u32[256]{0:T(256)S(1)}, u32[256]{0:T(256)}, u32[]{:S(2)}) copy-start(u32[256]{0:T(256)} %constant.193) | copy-start | bytes 3076
  85.2 18.5 %copy-start.29 = (f32[1,32]{1,0:T(1,128)S(1)}, f32[1,32]{1,0:T(1,128)}, u32[]{:S(2)}) copy-start(f32[1,32]{1,0:T(1,128)} %param.14) | copy-start | bytes 388
  85.2 18.7 %copy-start.30 = (f32[32]{0:T(128)S(1)}, f32[32]{0:T(128)}, u32[]{:S(2)}) copy-start(f32[32]{0:T(128)} %param.13) | copy-start | bytes 388
  85.2 327.6 %copy-start.28 = (f32[2048]{0:T(1024)S(1)}, f32[2048]{0:T(1024)}, u32[]{:S(2)}) copy-start(f32[2048]{0:T(1024)} %param.12) | copy-start | bytes 24580
  412.8 5.9 copy-start.12
  418.8 2.5 copy-start.25
  418.8 4.5 copy-start.13
  418.8 4.7 copy-start.23
  421.2 5.4 copy-start.2
  426.4 1.4 copy-start.14
  442.1 1.9 copy-start.1
  442.1 2.6 copy-start
  455.3 1.6 copy-start.5
  462.9 1.6 copy-start.4
  463.6 1.4 copy-start.10
  471.9 2.1 copy-start.8
  472.2 1.5 copy-start.6
  825.9 5.2 copy-start.18
  833.5 1.9 copy-start.17
  837.5 5.4 slice-start.4
  837.9 1.3 copy-start.22
  839.7 3.5 slice-start.5
  840.1 1.8 copy-start.7
  840.1 2.4 copy-start.9
  842.5 1.4 copy-start.20
  842.5 10.5 slice-start.2
  843.9 3.5 copy-start.21
  843.9 9.1 slice-start.3
  847.3 1.6 copy-start.11
  848.9 1.6 copy-start.3
  848.9 2.2 copy-start.15
  848.9 2.5 copy-start.26
  851.3 5.4 slice-start
  853.0 3.8 slice-start.1
  853.0 3.8 copy-start.16
  856.8 252.8 %copy-start.24 = (bf16[1,256,2048]{2,1,0:T(8,128)(2,1)S(1)}, bf16[1,256,2048]{2,1,0:T(8,128)(2,1)}, u32[]{:S(2)}) copy-start(bf16[1,256,2048]{2,1,0:T(8,128)(2,1)} %param.11) | copy-start | bytes 3145732
Sparse Core Ops, SparseCore 0:
  474.8 351.1 all-gather.4

commit v2 on v0

v2 whole, which is shorter than its diff:
```python
import jax
import jax.numpy as jnp
from jax import lax
from jax.sharding import PartitionSpec as P
from jax.experimental import pallas as pl
from jax.experimental.pallas import tpu as pltpu

EPSILON = 1e-06
MESH = pl.DeviceIdType.MESH
ORDERS = ("yxz", "zyx", "xzy")
AXIS_DIM = {"z": 0, "x": 1, "y": 2}
CHUNKS = 4
TOKENS = 256
WIDTH = 2048
SPAN = WIDTH // CHUNKS
BLOCK = 256
STEPS = TOKENS // 8
LANES = 512
F32 = jnp.float32
BF16 = jnp.bfloat16
NT = (((1,), (1,)), ((), ()))


class Place:
    def __init__(self):
        seq = lax.axis_index("seq")
        batch = lax.axis_index("batch")
        self.seq, self.batch = seq, batch
        self.at = {"z": seq // 16, "x": lax.rem(seq // 4, 4), "y": lax.rem(seq, 4)}
        self.z_hi = batch // 2
        self.core = lax.rem(batch, 2)

    def device(self, z, x, y, z_hi, core):
        return (z * 16 + x * 4 + y, z_hi * 2 + core)

    def line(self, axis, step):
        at = dict(self.at)
        at[axis] = lax.rem(at[axis] + 4 + step, 4)
        return self.device(at["z"], at["x"], at["y"], self.z_hi, self.core)

    def column(self, step, flip):
        full = lax.rem(self.z_hi * 4 + self.at["z"] + 8 + step, 8)
        core = lax.rem(self.core + flip, 2)
        return self.device(lax.rem(full, 4), self.at["x"], self.at["y"], full // 4, core)

    def ring(self, axis, step):
        return self.column(step, 0) if axis == "z" else self.line(axis, step)

    def sibling(self):
        return self.column(0, 1)


def remote(src, dst, send_sem, recv_sem, device):
    return pltpu.make_async_remote_copy(
        src_ref=src, dst_ref=dst, send_sem=send_sem, recv_sem=recv_sem, device_id=device, device_id_type=MESH
    )


class Weights:
    def __init__(self, place, buffer, send_sem, recv_sem, sib_send, sib_recv):
        self.place, self.buffer = place, buffer
        self.sems, self.sib_sems = (send_sem, recv_sem), (sib_send, sib_recv)

    def slab(self, w, phase, step, which, q, part):
        index = [None, None, None]
        for position, axis in enumerate(ORDERS[w]):
            own_at = self.place.at[axis]
            if position < phase:
                index[AXIS_DIM[axis]] = slice(None)
            elif position == phase:
                index[AXIS_DIM[axis]] = lax.rem(own_at + 4 + step, 4)
            else:
                index[AXIS_DIM[axis]] = own_at
        start, width = 0, WIDTH
        if phase == 2 and w == 0:
            index[AXIS_DIM["x"]] = q
        elif phase == 2:
            start, width = q * SPAN, SPAN
        if part is not None:
            width = width // 2
            start = start + part * width
        return self.buffer.at[w, index[0], index[1], index[2], which, :, pl.ds(start, width)]

    def piece(self, w, phase, kind, q, which, outgoing):
        right = kind % 2 == 0
        if kind < 2:
            step, part = (0 if outgoing else (-1 if right else 1)), None
        else:
            step, part = ((-1 if right else 1) if outgoing else 2), kind - 2
        return self.slab(w, phase, step, which, q, part)

    def hop(self, w, phase, kind, q, outgoing):
        ref = self.piece(w, phase, kind, q, self.place.core, outgoing)
        device = self.place.ring(ORDERS[w][phase], 1 if kind % 2 == 0 else -1)
        at = (w, phase, kind, q)
        return remote(ref, ref, self.sems[0].at[at], self.sems[1].at[at], device)

    def share(self, w, phase, kind, q, mine):
        ref = self.piece(w, phase, kind, q, self.place.core if mine else 1 - self.place.core, False)
        at = (w, phase, kind, q)
        return remote(ref, ref, self.sib_sems[0].at[at], self.sib_sems[1].at[at], self.place.sibling())

    def open(self, phase, q):
        for w in range(3):
            for kind in (0, 1):
                self.hop(w, phase, kind, q, True).start()

    def near(self, phase, q):
        for w in range(3):
            for kind in (0, 1):
                self.hop(w, phase, kind, q, False).wait_recv()
                self.hop(w, phase, kind + 2, q, True).start()
                self.share(w, phase, kind, q, True).start()

    def far(self, phase, q):
        for w in range(3):
            for kind in (2, 3):
                self.hop(w, phase, kind, q, False).wait_recv()
                self.share(w, phase, kind, q, True).start()

    def shared(self, w, phase, q):
        for kind in range(4):
            self.share(w, phase, kind, q, False).wait_recv()

    def drain(self, phase, q):
        for w in range(3):
            for kind in range(4):
                self.hop(w, phase, kind, q, True).wait_send()
                self.share(w, phase, kind, q, True).wait_send()


class LineExchange:
    def __init__(self, place, axis, ref_of, send_sem, recv_sem, level):
        self.place, self.axis, self.ref_of = place, axis, ref_of
        self.sems, self.level = (send_sem, recv_sem), level

    def copy(self, step, outgoing):
        at = self.place.at[self.axis]
        ref = self.ref_of(at if outgoing else lax.rem(at + 4 - step, 4))
        sem = (self.level, step - 1)
        return remote(ref, ref, self.sems[0].at[sem], self.sems[1].at[sem], self.place.line(self.axis, step))

    def start(self):
        for step in (1, 2, 3):
            self.copy(step, True).start()

    def arrive(self):
        for step in (1, 2, 3):
            self.copy(step, False).wait_recv()

    def drain(self):
        for step in (1, 2, 3):
            self.copy(step, True).wait_send()


def kernel(
    x_ref, g_ref, gain_ref, small_ref, gate_w, cand_w, out_w,
    layer_ref, grad_ref, state_grad_ref, bias_grad_ref,
    weights, smalls, pair, x_p, g_p, normed, inverse, retain, update, cand, back, factor,
    states, gate_g, cand_g, seg_keep, seg_end, seg_carry, enter, leave, sums, vectors, bias_acc,
    red0, red_in, red_x, red_y,
    own_sem, send_sem, recv_sem, sib_send, sib_recv, small_send, small_recv, sum_send, sum_recv,
    red_send, red_recv, last_send, last_recv,
):
    place = Place()
    core = place.core
    z, x, y = place.at["z"], place.at["x"], place.at["y"]
    shards = (out_w, gate_w, cand_w)
    own = []
    for w in range(3):
        for half in range(2):
            copy = pltpu.make_async_copy(
                shards[w].at[pl.ds(16 * half, 16), :], weights.at[w, z, x, y, half], own_sem.at[w, half]
            )
            copy.start()
            own.append(copy)
    lane = lax.broadcasted_iota(jnp.int32, (2, 128), 1)
    smalls[z, x, y] = jnp.where(lane // 32 == y, small_ref[...], 0.0)

    barrier = pltpu.get_barrier_semaphore()
    peers = [place.line(a, d) for a in "xy" for d in (1, 2, 3)]
    peers += [place.column(dz, dc) for dz in range(8) for dc in range(2) if dz or dc]
    for peer in peers:
        pl.semaphore_signal(barrier, inc=1, device_id=peer, device_id_type=MESH)
    pl.semaphore_wait(barrier, len(peers))
    for copy in own:
        copy.wait()

    gather = Weights(place, weights, send_sem, recv_sem, sib_send, sib_recv)
    small_lines = [
        LineExchange(place, "y", lambda v: smalls.at[z, x, v], small_send, small_recv, 0),
        LineExchange(place, "x", lambda v: smalls.at[z, v], small_send, small_recv, 1),
        LineExchange(place, "z", lambda v: smalls.at[v], small_send, small_recv, 2),
    ]

    def blocks(body):
        @pl.loop(0, WIDTH // BLOCK)
        def _(n):
            body(pl.ds(pl.multiple_of(n * BLOCK, BLOCK), BLOCK), n)

    row = lax.broadcasted_iota(jnp.int32, (TOKENS, TOKENS), 0)
    column = lax.broadcasted_iota(jnp.int32, (TOKENS, TOKENS), 1)

    gather.open(0, 0)
    small_lines[0].start()
    gather.near(0, 0)
    small_lines[0].arrive()
    small_lines[1].start()
    gather.far(0, 0)
    gather.open(1, 0)
    permute = jnp.where(column == lax.rem(row, 8) * STEPS + row // 8, 1.0, 0.0).astype(BF16)

    inverse[...] = jnp.zeros_like(inverse)

    def prepare(cols, n):
        rows = jnp.dot(permute, x_ref[:, cols], preferred_element_type=F32)
        x_p[:, cols] = rows.astype(BF16)
        inverse[...] += jnp.sum(rows * rows, axis=1, keepdims=True)
        g_p[:, cols] = jnp.dot(permute, g_ref[:, cols], preferred_element_type=F32).astype(BF16)

    blocks(prepare)
    gather.near(1, 0)
    small_lines[1].arrive()
    small_lines[2].start()
    gather.far(1, 0)

    gather.open(2, 0)
    gather.open(2, 1)
    inverse[...] = lax.rsqrt(inverse[...] * (1.0 / WIDTH) + EPSILON)

    def normalise(cols, n):
        normed[:, cols] = (x_p[:, cols].astype(F32) * inverse[...] * gain_ref[:, cols]).astype(BF16)

    blocks(normalise)
    small_lines[2].arrive()
    for i in range(4):
        for j in range(4):
            pair[:, pl.ds((4 * i + j) * 128, 128)] = (
                smalls[i, j, 0] + smalls[i, j, 1] + smalls[i, j, 2] + smalls[i, j, 3]
            )
    for w in range(3):
        for phase in range(2):
            gather.shared(w, phase, 0)

    def forward_scan(lo):
        lanes = pl.ds(lo, LANES)
        bias = pair[0:1, lanes]

        def step(i, carry):
            reach, state = carry
            rows = pl.ds(pl.multiple_of(i * 8, 8), 8)
            gate = retain[rows, lanes] + bias
            fade = jnp.exp(-jnp.abs(gate))
            high = 1.0 / (1.0 + fade)
            low = fade * high
            up = gate >= 0.0
            u = jnp.where(up, high, low)
            r = jnp.where(up, low, high)
            update[rows, lanes] = u
            retain[rows, lanes] = r
            return reach * r, r * state + u * cand[rows, lanes]

        start = (jnp.ones((8, LANES), F32), jnp.zeros((8, LANES), F32))
        reach, state = lax.fori_loop(0, STEPS, step, start, unroll=4)
        seg_keep[:, lanes] = reach
        seg_end[:, lanes] = state

    def chunk(q):
        gather.shared(1, 2, q)
        gather.shared(2, 2, q)

        @pl.loop(0, SPAN // BLOCK)
        def _(n):
            cols = pl.ds(pl.multiple_of(q * SPAN + n * BLOCK, BLOCK), BLOCK)
            for w, dst in ((1, retain), (2, cand)):
                block = weights[w, :, :, :, :, :, cols].reshape(WIDTH, BLOCK)
                dst[:, cols] = jnp.dot(normed[...], block, preferred_element_type=F32).astype(BF16).astype(F32)

        forward_scan(q * SPAN)
        gather.shared(0, 2, q)

        @pl.loop(0, 2)
        def _(n):
            block = weights[0, pl.ds(2 * n, 2), q].reshape(BLOCK, WIDTH)
            rows = lax.dot_general(g_p[...], block, NT, preferred_element_type=F32).astype(BF16).astype(F32)
            lo = pl.multiple_of(n * 1024 + q * 128, 128)
            back[:, pl.ds(lo, 128)] = rows[:, :128]
            back[:, pl.ds(pl.multiple_of(lo + 512, 128), 128)] = rows[:, 128:]

    for q in range(CHUNKS + 2):
        if q < CHUNKS:
            gather.near(2, q)
            if q + 2 < CHUNKS:
                gather.open(2, q + 2)
        if 1 <= q <= CHUNKS:
            gather.far(2, q - 1)
        if q >= 2:
            chunk(q - 2)

    for lo in range(0, WIDTH, LANES):
        lanes = pl.ds(lo, LANES)

        def step(i, carry):
            rows = pl.ds(pl.multiple_of((STEPS - 1 - i) * 8, 8), 8)
            return retain[rows, lanes] * (back[rows, lanes] + carry)

        seg_carry[:, lanes] = lax.fori_loop(0, STEPS, step, jnp.zeros((8, LANES), F32), unroll=4)

    keep, end, carry = seg_keep[0:1], seg_end[0:1], seg_carry[7:8]
    for k in range(1, 8):
        end = seg_keep[k : k + 1] * end + seg_end[k : k + 1]
        keep = keep * seg_keep[k : k + 1]
        carry = seg_carry[7 - k : 8 - k] + seg_keep[7 - k : 8 - k] * carry
    total = (keep, end, carry)
    lines = []
    for level, axis in enumerate("yxz"):
        at = place.at[axis]
        for k in range(3):
            sums[level, at, k : k + 1, :] = total[k]
        line = LineExchange(place, axis, lambda v, level=level: sums.at[level, v], sum_send, sum_recv, level)
        line.start()
        line.arrive()
        lines.append(line)
        keeps = [sums[level, m, 0:1, :] for m in range(4)]
        ends = [sums[level, m, 1:2, :] for m in range(4)]
        carries = [sums[level, m, 2:3, :] for m in range(4)]
        one, zero = jnp.ones((1, WIDTH), F32), jnp.zeros((1, WIDTH), F32)
        before, arrived, after, returned = one, zero, one, zero
        for m in range(3):
            take = m < at
            arrived = jnp.where(take, keeps[m] * arrived + ends[m], arrived)
            before = jnp.where(take, keeps[m] * before, before)
        for m in (3, 2, 1):
            take = m > at
            returned = jnp.where(take, carries[m] + keeps[m] * returned, returned)
            after = jnp.where(take, keeps[m] * after, after)
        for k, value in enumerate((before, arrived, after, returned)):
            vectors[4 * level + k] = value
        keep, end, carry = keeps[0], ends[0], carries[3]
        for m in range(1, 4):
            end = keeps[m] * end + ends[m]
            keep = keep * keeps[m]
            carry = carries[3 - m] + keeps[3 - m] * carry
        total = (keep, end, carry)
    vectors[12] = total[2]
    entering, leaving = pair[1:2, :], jnp.zeros((1, WIDTH), F32)
    for level in (2, 1, 0):
        entering = vectors[4 * level] * entering + vectors[4 * level + 1]
        leaving = vectors[4 * level + 2] * leaving + vectors[4 * level + 3]
    for k in range(8):
        enter[k : k + 1, :] = entering
        leave[7 - k : 8 - k, :] = leaving
        if k < 7:
            entering = seg_keep[k : k + 1] * entering + seg_end[k : k + 1]
            leaving = seg_keep[7 - k : 8 - k] * leaving + seg_carry[7 - k : 8 - k]
    own_lanes = pl.ds(pl.multiple_of((z * 4 + x) * 128, 128), 128)
    turn = lax.rem(128 - 32 * y, 128)
    state_grad_ref[...] = pltpu.roll(vectors[12, :, own_lanes], turn, 1)[:, :32]

    for lo in range(0, WIDTH, LANES):
        lanes = pl.ds(lo, LANES)

        def step(i, state):
            halves = []
            for k in range(2):
                rows = pl.ds(pl.multiple_of(i * 16 + k * 8, 8), 8)
                r, u, c = retain[rows, lanes], update[rows, lanes], cand[rows, lanes]
                factor[rows, lanes] = (c - state) * u * r
                state = r * state + u * c
                halves.append(state)
            states[pl.ds(pl.multiple_of(i * 16, 16), 16), lanes] = jnp.concatenate(halves, axis=0).astype(BF16)
            return state

        lax.fori_loop(0, STEPS // 2, step, enter[:, lanes], unroll=2)

    for lo in range(0, WIDTH, LANES):
        lanes = pl.ds(lo, LANES)

        def step(i, carry):
            coming, total_bias = carry
            gates, cands = [None, None], [None, None]
            for k in (1, 0):
                rows = pl.ds(pl.multiple_of((STEPS // 2 - 1 - i) * 16 + k * 8, 8), 8)
                carried = back[rows, lanes] + coming
                gates[k] = carried * factor[rows, lanes]
                cands[k] = carried * update[rows, lanes]
                coming = retain[rows, lanes] * carried
                total_bias = total_bias + gates[k]
            rows = pl.ds(pl.multiple_of((STEPS // 2 - 1 - i) * 16, 16), 16)
            gate_g[rows, lanes] = jnp.concatenate(gates, axis=0).astype(BF16)
            cand_g[rows, lanes] = jnp.concatenate(cands, axis=0).astype(BF16)
            return coming, total_bias

        start = (leave[:, lanes], jnp.zeros((8, LANES), F32))
        _, total_bias = lax.fori_loop(0, STEPS // 2, step, start, unroll=2)
        bias_acc[:, lanes] = jnp.sum(total_bias, axis=0, keepdims=True)

    for i in range(4):
        for j in range(4):
            red0[i, j : j + 1, :] = bias_acc[:, pl.ds((4 * i + j) * 128, 128)]

    def reduce_copy(dz, dc):
        k = dz * 2 + dc
        return remote(
            red0.at[lax.rem(z + dz, 4)], red_in.at[k], red_send.at[k], red_recv.at[k], place.column(dz, dc)
        )

    column_peers = [(dz, dc) for dz in range(8) for dc in range(2) if dz or dc]
    for dz, dc in column_peers:
        reduce_copy(dz, dc).start()

    restore = jnp.where(row == lax.rem(column, 8) * STEPS + column // 8, 1.0, 0.0).astype(BF16)

    def layer(cols, n):
        block = weights[0, :, :, :, :, :, cols].reshape(WIDTH, BLOCK)
        rows = x_p[:, cols].astype(F32) + jnp.dot(states[...], block, preferred_element_type=F32)
        layer_ref[:, cols] = jnp.dot(restore, rows.astype(BF16), preferred_element_type=F32).astype(BF16)

    blocks(layer)

    for dz, dc in column_peers:
        reduce_copy(dz, dc).wait_recv()
    part = red0[z]
    for dz, dc in column_peers:
        part = part + red_in[dz * 2 + dc]
    for j in range(4):
        red_x[0, j] = part[j : j + 1, :]

    def copy_x(step):
        return remote(
            red_x.at[0, lax.rem(x + step, 4)], red_x.at[step, 0], last_send.at[0, step - 1],
            last_recv.at[0, step - 1], place.line("x", step),
        )

    for step in (1, 2, 3):
        copy_x(step).start()

    inverse_rows = inverse[...]
    row_sum = jnp.zeros((TOKENS, 1), F32)

    def unit_block(n, row_sum):
        cols = pl.ds(pl.multiple_of(n * BLOCK, BLOCK), BLOCK)
        which = pl.ds(2 * lax.rem(n, 2), 2)
        gate_block = weights[1, n // 2, which].reshape(BLOCK, WIDTH)
        cand_block = weights[2, n // 2, which].reshape(BLOCK, WIDTH)
        rows = lax.dot_general(gate_g[...], gate_block, NT, preferred_element_type=F32)
        rows = rows + lax.dot_general(cand_g[...], cand_block, NT, preferred_element_type=F32)
        rows = rows * gain_ref[:, cols]
        factor[:, cols] = rows
        unit = x_p[:, cols].astype(F32) * inverse_rows
        return row_sum + jnp.sum(rows * unit, axis=1, keepdims=True)

    row_sum = lax.fori_loop(0, 4, unit_block, row_sum)
    for step in (1, 2, 3):
        copy_x(step).wait_recv()
    red_y[y] = red_x[0, x] + red_x[1, 0] + red_x[2, 0] + red_x[3, 0]
    last_line = LineExchange(place, "y", lambda v: red_y.at[v], last_send, last_recv, 1)
    last_line.start()
    row_sum = lax.fori_loop(4, 8, unit_block, row_sum)
    last_line.arrive()
    bias_total = red_y[0] + red_y[1] + red_y[2] + red_y[3]
    bias_grad_ref[...] = pltpu.roll(bias_total, turn, 1)[:, :32]
    mean = row_sum * (1.0 / WIDTH)

    def finish(cols, n):
        unit = x_p[:, cols].astype(F32) * inverse_rows
        rows = g_p[:, cols].astype(F32) + inverse_rows * (factor[:, cols] - unit * mean)
        grad_ref[:, cols] = jnp.dot(restore, rows.astype(BF16), preferred_element_type=F32).astype(BF16)

    blocks(finish)

    for phase in range(3):
        for q in range(CHUNKS if phase == 2 else 1):
            gather.drain(phase, q)
    for line in small_lines + lines + [last_line]:
        line.drain()
    for dz, dc in column_peers:
        reduce_copy(dz, dc).wait_send()
    for step in (1, 2, 3):
        copy_x(step).wait_send()


def on_device(inputs, output_grad, norm_gain, gate_bias, state_in, w_gate, w_cand, w_out):
    small = jnp.stack([jnp.tile(gate_bias, 4), jnp.tile(state_in[0], 4)])
    whole = lambda rows, dtype: pltpu.VMEM((rows, WIDTH), dtype)
    dma = pltpu.SemaphoreType.DMA
    layer, grad, state_grad, bias_grad = pl.pallas_call(
        kernel,
        out_shape=(
            jax.ShapeDtypeStruct((TOKENS, WIDTH), BF16),
            jax.ShapeDtypeStruct((TOKENS, WIDTH), BF16),
            jax.ShapeDtypeStruct((1, 32), F32),
            jax.ShapeDtypeStruct((1, 32), F32),
        ),
        in_specs=[pl.BlockSpec(memory_space=pltpu.VMEM)] * 7,
        out_specs=[pl.BlockSpec(memory_space=pltpu.VMEM)] * 4,
        scratch_shapes=[
            pltpu.VMEM((3, 4, 4, 4, 2, 16, WIDTH), BF16),
            pltpu.VMEM((4, 4, 4, 2, 128), F32),
            whole(2, F32),
            whole(TOKENS, BF16), whole(TOKENS, BF16), whole(TOKENS, BF16),
            pltpu.VMEM((TOKENS, 1), F32),
            whole(TOKENS, F32), whole(TOKENS, F32), whole(TOKENS, F32), whole(TOKENS, F32), whole(TOKENS, F32),
            whole(TOKENS, BF16), whole(TOKENS, BF16), whole(TOKENS, BF16),
            whole(8, F32), whole(8, F32), whole(8, F32), whole(8, F32), whole(8, F32),
            pltpu.VMEM((3, 4, 4, WIDTH), F32),
            pltpu.VMEM((13, 1, WIDTH), F32),
            whole(1, F32),
            pltpu.VMEM((4, 4, 128), F32),
            pltpu.VMEM((16, 4, 128), F32),
            pltpu.VMEM((4, 4, 1, 128), F32),
            pltpu.VMEM((4, 1, 128), F32),
            dma((3, 2)),
            dma((3, 3, 4, CHUNKS)), dma((3, 3, 4, CHUNKS)), dma((3, 3, 4, CHUNKS)), dma((3, 3, 4, CHUNKS)),
            dma((3, 3)), dma((3, 3)), dma((3, 3)), dma((3, 3)),
            dma((16,)), dma((16,)), dma((2, 3)), dma((2, 3)),
        ],
        compiler_params=pltpu.CompilerParams(
            collective_id=0, has_side_effects=True, vmem_limit_bytes=62 * 1024 * 1024
        ),
        name="mixer",
    )(inputs[0], output_grad[0], norm_gain[None], small, w_gate, w_cand, w_out)
    return (layer[None], grad[None], state_grad, bias_grad[0])


def solution(mesh):
    return jax.shard_map(
        on_device,
        mesh=mesh,
        in_specs=(
            P("batch", "seq", None),
            P("batch", "seq", None),
            P(),
            P("seq"),
            P("batch", "seq"),
            P("seq", None),
            P("seq", None),
            P("seq", None),
        ),
        out_specs=(P("batch", "seq", None), P("batch", "seq", None), P("batch", "seq"), P("seq")),
        check_vma=False,
    )
```

time: 1310 us -> 117 us (0.09)
  waiting for transfers between devices: 1050 us -> 0 us
  Pallas kernels: 0 us -> 110 us
  blocking collectives: 58.4 us -> 0 us
  other arithmetic: 57.8 us -> 0.57 us
  starting transfers between devices: 46.1 us -> 0 us
  matrix products: 39 us -> 0 us
  local copies, waits for them, and re-layouts: 36 us -> 5.93 us
  between operations: 14.9 us -> 0.66 us
    all_gather x3 -> x0, waiting for transfers between devices: 1010 us -> none  [the longest x1 346 us: on_device(): lax.all_gather(w_out, 'seq', axis=0, tiled=True)]
    pallas_call x0 -> x1, Pallas kernels: none -> 110 us  [on_device(): pl.pallas_call(kernel, out_shape=(jax.ShapeDtypeStruct((TOKENS, WIDTH), B...]
    psum x1 -> x0, blocking collectives: 58.4 us -> none  [on_device(): bias_grad = lax.psum(bias_part, 'batch')]
    all_to_all x6 -> x0, starting transfers between devices: 46 us -> none  [the longest x1 10.6 us: on_device(): lax.all_to_all(states.astype(jnp.bfloat16), 'seq', split_axis=1, concat_a...]
    add x25 -> x0, other arithmetic: 40.3 us -> none  [shift_scan(): drive = keep * drive_far + drive]
    all_to_all x6 -> x0, waiting for transfers between devices: 39.9 us -> none  [the longest x1 14.3 us: on_device(): lax.all_to_all(back_grads, 'seq', split_axis=0, concat_axis=1, tiled=True)]
    dot_general x6 -> x0, matrix products: 39 us -> none  [the longest x1 6.74 us: on_device(): lax.dot_general(out_full, grad_rows, (((1,), (1,)), ((), ())), preferred_...]
    slice x40 -> x0, local copies, waits for them, and re-layouts: 16.5 us -> none  [the longest x26 12.3 us: shifted(): kept = lax.slice_in_dim(values, offset, length, 1, axis)]
  transfers between devices with their start and end apart: 9 -> 0, of which waited for: 6 -> 0; matrix products, arithmetic and copies ran while one was open for 4% -> 0% of each run, Pallas kernels for 0% -> 0%
where the time goes in v2:
time: 117 us
  Pallas kernels  110 us (94%)
  local copies, waits for them, and re-layouts  5.93 us (5%)
    pallas_call x1, Pallas kernels, on_device(): pl.pallas_call(kernel, out_shape=(jax.ShapeDtypeStruct((TOKENS, WIDTH), B...  110 us
    unnamed x14, local copies, waits for them, and re-layouts  5.76 us

profile of v2, /device:TPU:1, one launch (start us, length us, event | category | flops | bytes accessed | tf_op | source)
XLA Modules:
  0.0 117.2 jit_solution(15300569317066007343)
XLA Ops:
  0.6 0.0 copy-start.1
  0.6 0.6 copy-done.1
  1.3 0.0 copy-start.2
  1.3 0.1 stack_tile.6
  1.4 0.6 copy-done.2
  1.9 0.1 stack_tile.7
  2.0 0.6 pad_maximum_fusion.small_ref
  2.6 110.0 %mixer.1 = (bf16[256,2048]{1,0:T(8,128)(2,1)}, bf16[256,2048]{1,0:T(8,128)(2,1)}, f32[1,32]{1,0:T(1,128)}, f32[1,32]{1,0:T(1,128)}) custom-call(bf16[256,2048]{1,0:T(8,128)(2,1)} %bitcast.7, bf16[256,2048]{1,0:T(8,128)(2,1)} %bitcast.8, f32[1,2048]{1,0:T(1,128)} %bitcast.11, f32[2,128]{1,0:T(2,128)} %pad_maximum_fusion.small_ref, bf16[32,2048]{1,0:T(8,128)(2,1)} %gate_w.1, ...), custom_call_target="tpu_custom_call" | custom-call | tf_op jit(solution)/shard_map/mixer/pallas_call | solution.py:487
  112.6 0.0 copy-start
  112.6 2.4 %copy.16 = bf16[1,256,2048]{2,1,0:T(8,128)(2,1)} copy(bf16[1,256,2048]{2,1,0:T(8,128)(2,1)} %bitcast.10) | data formatting | bytes 2097152
  115.0 0.0 copy-done
  115.0 0.0 copy-start.4
  115.0 1.0 copy.17
  116.0 0.0 copy-done.4
  116.0 0.0 copy-start.3
  116.0 0.5 copy.18
  116.5 0.2 copy-done.3
  116.7 0.5 copy.19
  (2 shorter events, 0.0 us)
Async XLA Ops:
  0.6 0.7 copy-start.1
  1.3 0.7 copy-start.2
  112.6 2.4 %copy-start = (bf16[256,2048]{1,0:T(8,128)(2,1)S(1)}, bf16[256,2048]{1,0:T(8,128)(2,1)}, u32[]{:S(2)}) copy-start(bf16[256,2048]{1,0:T(8,128)(2,1)} %get-tuple-element.9) | copy-start | bytes 3145732
  115.0 1.0 copy-start.4
  116.0 0.7 copy-start.3

commit v3 on v2

v3 whole, which is shorter than its diff:
```python
import jax
import jax.numpy as jnp
from jax import lax
from jax.sharding import PartitionSpec as P
from jax.experimental import pallas as pl
from jax.experimental.pallas import tpu as pltpu

EPSILON = 1e-06
MESH = pl.DeviceIdType.MESH
ORDERS = ("xyz", "yzx", "zxy")
AXIS_DIM = {"z": 0, "x": 1, "y": 2}
CHUNKS = 4
TOKENS = 256
WIDTH = 2048
SPAN = WIDTH // CHUNKS
BLOCK = 512
STEPS = TOKENS // 8
UNROLL = 32
LANES = 512
F32 = jnp.float32
BF16 = jnp.bfloat16
NT = (((1,), (1,)), ((), ()))


class Place:
    def __init__(self):
        seq = lax.axis_index("seq")
        batch = lax.axis_index("batch")
        self.seq, self.batch = seq, batch
        self.at = {"z": seq // 16, "x": lax.rem(seq // 4, 4), "y": lax.rem(seq, 4)}
        self.z_hi = batch // 2
        self.core = lax.rem(batch, 2)

    def device(self, z, x, y, z_hi, core):
        return (z * 16 + x * 4 + y, z_hi * 2 + core)

    def line(self, axis, step):
        at = dict(self.at)
        at[axis] = lax.rem(at[axis] + 4 + step, 4)
        return self.device(at["z"], at["x"], at["y"], self.z_hi, self.core)

    def column(self, step, flip):
        full = lax.rem(self.z_hi * 4 + self.at["z"] + 8 + step, 8)
        core = lax.rem(self.core + flip, 2)
        return self.device(lax.rem(full, 4), self.at["x"], self.at["y"], full // 4, core)

    def ring(self, axis, step):
        return self.column(step, 0) if axis == "z" else self.line(axis, step)

    def sibling(self):
        return self.column(0, 1)


def remote(src, dst, send_sem, recv_sem, device):
    return pltpu.make_async_remote_copy(
        src_ref=src, dst_ref=dst, send_sem=send_sem, recv_sem=recv_sem, device_id=device, device_id_type=MESH
    )


class Weights:
    def __init__(self, place, buffer, send_sem, recv_sem, sib_send, sib_recv):
        self.place, self.buffer = place, buffer
        self.sems, self.sib_sems = (send_sem, recv_sem), (sib_send, sib_recv)

    def slab(self, w, phase, step, which, q, part, prev=None):
        index = [None, None, None]
        for position, axis in enumerate(ORDERS[w]):
            own_at = self.place.at[axis]
            if position == phase - 1 and prev is not None:
                index[AXIS_DIM[axis]] = lax.rem(own_at + 4 + prev, 4)
            elif position < phase:
                index[AXIS_DIM[axis]] = slice(None)
            elif position == phase:
                index[AXIS_DIM[axis]] = lax.rem(own_at + 4 + step, 4)
            else:
                index[AXIS_DIM[axis]] = own_at
        start, width = 0, WIDTH
        if phase == 2 and w == 0:
            index[AXIS_DIM["x"]] = q
        elif phase == 2:
            start, width = q * SPAN, SPAN
        if part is not None:
            width = width // 2
            start = start + part * width
        return self.buffer.at[w, index[0], index[1], index[2], which, :, pl.ds(start, width)]

    def piece(self, w, phase, kind, q, which, outgoing):
        right = kind % 2 == 0
        if kind < 2:
            step, part = (0 if outgoing else (-1 if right else 1)), None
        else:
            step, part = ((-1 if right else 1) if outgoing else 2), kind - 2
        return self.slab(w, phase, step, which, q, part)

    def copy(self, ref, w, phase, kind, q):
        device = self.place.ring(ORDERS[w][phase], 1 if kind % 2 == 0 else -1)
        at = (w, phase, kind, q)
        return remote(ref, ref, self.sems[0].at[at], self.sems[1].at[at], device)

    def hop(self, w, phase, kind, q, outgoing):
        return self.copy(self.piece(w, phase, kind, q, self.place.core, outgoing), w, phase, kind, q)

    def share(self, w, phase, kind, q, mine):
        ref = self.piece(w, phase, kind, q, self.place.core if mine else 1 - self.place.core, False)
        at = (w, phase, kind, q)
        return remote(ref, ref, self.sib_sems[0].at[at], self.sib_sems[1].at[at], self.place.sibling())

    def part(self, w, phase, q, prev):
        for kind in (0, 1):
            self.copy(self.slab(w, phase, 0, self.place.core, q, None, prev), w, phase, kind, q).start()

    def open(self):
        for w in range(3):
            for kind in (0, 1):
                self.hop(w, 0, kind, 0, True).start()
        for w in range(3):
            self.part(w, 1, 0, 0)

    def near(self, phase, q):
        ahead = {0: (0,), 1: (0, 1), 2: ()}[phase]
        for w in range(3):
            for kind in (0, 1):
                self.hop(w, phase, kind, q, False).wait_recv()
                self.hop(w, phase, kind + 2, q, True).start()
                self.share(w, phase, kind, q, True).start()
                for later in ahead:
                    self.part(w, phase + 1, later, 1 if kind else -1)

    def far(self, phase, q):
        for w in range(3):
            for kind in (2, 3):
                self.hop(w, phase, kind, q, False).wait_recv()
                self.share(w, phase, kind, q, True).start()
            if phase == 0:
                self.part(w, 1, 0, 2)
            if phase == 1:
                for later in (0, 1):
                    self.part(w, 2, later, 2)
        if phase == 0:
            for later in range(CHUNKS):
                for w in range(3):
                    self.part(w, 2, later, 0)

    def rest(self, q, prevs):
        for w in range(3):
            for prev in prevs:
                self.part(w, 2, q, prev)

    def shared(self, w, phase, q):
        for kind in range(4):
            self.share(w, phase, kind, q, False).wait_recv()

    def drain(self, phase, q):
        for w in range(3):
            for kind in range(4):
                self.hop(w, phase, kind, q, True).wait_send()
                self.share(w, phase, kind, q, True).wait_send()


class LineExchange:
    def __init__(self, place, axis, ref_of, send_sem, recv_sem, level):
        self.place, self.axis, self.ref_of = place, axis, ref_of
        self.sems, self.level = (send_sem, recv_sem), level

    def copy(self, step, outgoing):
        at = self.place.at[self.axis]
        ref = self.ref_of(at if outgoing else lax.rem(at + 4 - step, 4))
        sem = (self.level, step - 1)
        return remote(ref, ref, self.sems[0].at[sem], self.sems[1].at[sem], self.place.line(self.axis, step))

    def start(self):
        for step in (1, 2, 3):
            self.copy(step, True).start()

    def arrive(self):
        for step in (1, 2, 3):
            self.copy(step, False).wait_recv()

    def drain(self):
        for step in (1, 2, 3):
            self.copy(step, True).wait_send()


def kernel(
    x_hbm, g_hbm, gain_ref, bias_ref, state_ref, gate_w, cand_w, out_w,
    layer_ref, grad_ref, state_grad_ref, bias_grad_ref,
    weights, smalls, pair, x_in, g_in, x_p, g_p, normed, inverse, retain, update, cand, back, factor,
    states, gate_g, cand_g, layer_acc, grad_acc, seg_keep, seg_end, seg_carry, enter, leave, sums, vectors, bias_acc,
    red0, red_in, red_x, red_y,
    own_sem, in_sem, send_sem, recv_sem, sib_send, sib_recv, small_send, small_recv, sum_send, sum_recv,
    red_send, red_recv, last_send, last_recv,
):
    place = Place()
    z, x, y = place.at["z"], place.at["x"], place.at["y"]
    barrier = pltpu.get_barrier_semaphore()
    column_peers = [(dz, dc) for dz in range(8) for dc in range(2) if dz or dc]
    peers = [place.line(a, d) for a in "xy" for d in (1, 2, 3)]
    peers += [place.column(dz, dc) for dz, dc in column_peers]
    for peer in peers:
        pl.semaphore_signal(barrier, inc=1, device_id=peer, device_id_type=MESH)

    read_x = pltpu.make_async_copy(x_hbm, x_in, in_sem.at[0])
    read_g = pltpu.make_async_copy(g_hbm, g_in, in_sem.at[1])
    own = [pltpu.make_async_copy(w, weights.at[k, z, x, y], own_sem.at[k]) for k, w in enumerate((out_w, gate_w, cand_w))]
    read_x.start()
    own[0].start()
    for k, w in ((1, gate_w), (2, cand_w)):
        for q in range(4):
            for i in range(4):
                pltpu.make_async_copy(
                    w.at[:, :, pl.ds((i * 4 + q) * 128, 128)],
                    weights.at[k, z, x, y, :, :, pl.ds((q * 4 + i) * 128, 128)],
                    own_sem.at[k],
                ).start()
    read_g.start()
    lane = lax.broadcasted_iota(jnp.int32, (2, 128), 1)
    small = [jnp.concatenate([ref[...]] * 4, axis=1) for ref in (bias_ref, state_ref)]
    smalls[z, x, y] = jnp.where(lane // 32 == y, jnp.concatenate(small, axis=0), 0.0)

    gather = Weights(place, weights, send_sem, recv_sem, sib_send, sib_recv)
    small_lines = [
        LineExchange(place, "y", lambda v: smalls.at[z, x, v], small_send, small_recv, 0),
        LineExchange(place, "x", lambda v: smalls.at[z, v], small_send, small_recv, 1),
        LineExchange(place, "z", lambda v: smalls.at[v], small_send, small_recv, 2),
    ]

    def blocks(body):
        @pl.loop(0, WIDTH // BLOCK)
        def _(n):
            body(pl.ds(pl.multiple_of(n * BLOCK, BLOCK), BLOCK), n)

    row = lax.broadcasted_iota(jnp.int32, (TOKENS, TOKENS), 0)
    column = lax.broadcasted_iota(jnp.int32, (TOKENS, TOKENS), 1)
    permute = jnp.where(column == lax.rem(row, 8) * STEPS + row // 8, 1.0, 0.0).astype(BF16)
    inverse[...] = jnp.zeros_like(inverse)

    def prepare(cols, n):
        rows = jnp.dot(permute, x_in[:, cols], preferred_element_type=F32)
        x_p[:, cols] = rows.astype(BF16)
        inverse[...] += jnp.sum(rows * rows, axis=1, keepdims=True)

    def prepare_grads(cols, n):
        g_p[:, cols] = jnp.dot(permute, g_in[:, cols], preferred_element_type=F32).astype(BF16)

    def normalise(cols, n):
        normed[:, cols] = (x_p[:, cols].astype(F32) * inverse[...] * gain_ref[:, cols]).astype(BF16)

    read_x.wait()
    blocks(prepare)
    inverse[...] = lax.rsqrt(inverse[...] * (1.0 / WIDTH) + EPSILON)
    for copy in own:
        copy.wait()
    pl.semaphore_wait(barrier, len(peers))

    small_lines[0].start()
    gather.open()
    read_g.wait()
    blocks(prepare_grads)
    small_lines[0].arrive()
    small_lines[1].start()
    gather.near(0, 0)
    gather.far(0, 0)
    blocks(normalise)
    small_lines[1].arrive()
    small_lines[2].start()
    gather.near(1, 0)
    gather.far(1, 0)

    def gather_pair():
        small_lines[2].arrive()
        for i in range(4):
            for j in range(4):
                pair[:, pl.ds((4 * j + i) * 128, 128)] = (
                    smalls[i, j, 0] + smalls[i, j, 1] + smalls[i, j, 2] + smalls[i, j, 3]
                )

    def stage_gates(q):
        gather.shared(1, 2, q)
        gather.shared(2, 2, q)
        lanes = pl.ds(q * SPAN, SPAN)
        for w, dst in ((1, retain), (2, cand)):
            block = weights[w, :, :, :, :, :, lanes].reshape(WIDTH, SPAN)
            dst[:, lanes] = jnp.dot(normed[...], block, preferred_element_type=F32).astype(BF16).astype(F32)

    def forward_scan(q):
        lanes = pl.ds(q * SPAN, SPAN)
        bias = pair[0:1, lanes]

        def step(i, carry):
            reach, state = carry
            rows = pl.ds(pl.multiple_of(i * 8, 8), 8)
            gate = retain[rows, lanes] + bias
            fade = jnp.exp(-jnp.abs(gate))
            high = 1.0 / (1.0 + fade)
            low = fade * high
            up = gate >= 0.0
            u = jnp.where(up, high, low)
            r = jnp.where(up, low, high)
            update[rows, lanes] = u
            retain[rows, lanes] = r
            return reach * r, r * state + u * cand[rows, lanes]

        start = (jnp.ones((8, SPAN), F32), jnp.zeros((8, SPAN), F32))
        reach, state = lax.fori_loop(0, STEPS, step, start, unroll=UNROLL)
        seg_keep[:, lanes] = reach
        seg_end[:, lanes] = state

    def stage_back(q):
        gather.shared(0, 2, q)
        block = weights[0, :, q].reshape(SPAN, WIDTH)
        rows = lax.dot_general(g_p[...], block, NT, preferred_element_type=F32)
        back[:, pl.ds(q * SPAN, SPAN)] = rows.astype(BF16).astype(F32)

    def backward_scan(q):
        lanes = pl.ds(q * SPAN, SPAN)

        def step(i, carry):
            rows = pl.ds(pl.multiple_of((STEPS - 1 - i) * 8, 8), 8)
            return retain[rows, lanes] * (back[rows, lanes] + carry)

        seg_carry[:, lanes] = lax.fori_loop(0, STEPS, step, jnp.zeros((8, SPAN), F32), unroll=UNROLL)

    lines = [
        [
            LineExchange(
                place, axis, lambda v, level=level, q=q: sums.at[level, q, v], sum_send, sum_recv, level * CHUNKS + q
            )
            for q in range(CHUNKS)
        ]
        for level, axis in enumerate("yxz")
    ]

    def publish(level, q, total):
        at = place.at["yxz"[level]]
        for k in range(3):
            sums[level, q, at, k : k + 1, :] = total[k]
        lines[level][q].start()

    def summarise(q):
        lanes = pl.ds(q * SPAN, SPAN)
        keeps, ends, carries = seg_keep[:, lanes], seg_end[:, lanes], seg_carry[:, lanes]
        keep, end, carry = keeps[0:1], ends[0:1], carries[7:8]
        for k in range(1, 8):
            end = keeps[k : k + 1] * end + ends[k : k + 1]
            keep = keep * keeps[k : k + 1]
            carry = carries[7 - k : 8 - k] + keeps[7 - k : 8 - k] * carry
        publish(0, q, (keep, end, carry))

    def compose(level, q):
        at = place.at["yxz"[level]]
        lines[level][q].arrive()
        keeps = [sums[level, q, m, 0:1, :] for m in range(4)]
        ends = [sums[level, q, m, 1:2, :] for m in range(4)]
        carries = [sums[level, q, m, 2:3, :] for m in range(4)]
        keep, end, carry = keeps[0], ends[0], carries[3]
        for m in range(1, 4):
            end = keeps[m] * end + ends[m]
            keep = keep * keeps[m]
            carry = carries[3 - m] + keeps[3 - m] * carry
        if level < 2:
            publish(level + 1, q, (keep, end, carry))
        else:
            vectors[q, 12] = carry
        one, zero = jnp.ones((1, SPAN), F32), jnp.zeros((1, SPAN), F32)
        before, arrived, after, returned = one, zero, one, zero
        for m in range(3):
            take = m < at
            arrived = jnp.where(take, keeps[m] * arrived + ends[m], arrived)
            before = jnp.where(take, keeps[m] * before, before)
        for m in (3, 2, 1):
            take = m > at
            returned = jnp.where(take, carries[m] + keeps[m] * returned, returned)
            after = jnp.where(take, keeps[m] * after, after)
        for k, value in enumerate((before, arrived, after, returned)):
            vectors[q, 4 * level + k] = value

    def settle(q):
        lanes = pl.ds(q * SPAN, SPAN)
        entering, leaving = pair[1:2, lanes], jnp.zeros((1, SPAN), F32)
        for level in (2, 1, 0):
            entering = vectors[q, 4 * level] * entering + vectors[q, 4 * level + 1]
            leaving = vectors[q, 4 * level + 2] * leaving + vectors[q, 4 * level + 3]
        keeps, ends, carries = seg_keep[:, lanes], seg_end[:, lanes], seg_carry[:, lanes]
        for k in range(8):
            enter[k : k + 1, lanes] = entering
            leave[7 - k : 8 - k, lanes] = leaving
            if k < 7:
                entering = keeps[k : k + 1] * entering + ends[k : k + 1]
                leaving = keeps[7 - k : 8 - k] * leaving + carries[7 - k : 8 - k]

    def gradients(q):
        lanes = pl.ds(q * SPAN, SPAN)

        def ahead(i, state):
            halves = []
            for k in range(2):
                rows = pl.ds(pl.multiple_of(i * 16 + k * 8, 8), 8)
                r, u, c = retain[rows, lanes], update[rows, lanes], cand[rows, lanes]
                factor[rows, lanes] = (c - state) * u * r
                state = r * state + u * c
                halves.append(state)
            states[pl.ds(pl.multiple_of(i * 16, 16), 16), lanes] = jnp.concatenate(halves, axis=0).astype(BF16)
            return state

        lax.fori_loop(0, STEPS // 2, ahead, enter[:, lanes], unroll=2)

        def astern(i, carry):
            coming, total_bias = carry
            gates, cands = [None, None], [None, None]
            for k in (1, 0):
                rows = pl.ds(pl.multiple_of((STEPS // 2 - 1 - i) * 16 + k * 8, 8), 8)
                carried = back[rows, lanes] + coming
                gates[k] = carried * factor[rows, lanes]
                cands[k] = carried * update[rows, lanes]
                coming = retain[rows, lanes] * carried
                total_bias = total_bias + gates[k]
            rows = pl.ds(pl.multiple_of((STEPS // 2 - 1 - i) * 16, 16), 16)
            gate_g[rows, lanes] = jnp.concatenate(gates, axis=0).astype(BF16)
            cand_g[rows, lanes] = jnp.concatenate(cands, axis=0).astype(BF16)
            return coming, total_bias

        start = (leave[:, lanes], jnp.zeros((8, SPAN), F32))
        _, total_bias = lax.fori_loop(0, STEPS // 2, astern, start, unroll=2)
        bias_acc[:, lanes] = jnp.sum(total_bias, axis=0, keepdims=True)
        for i in range(4):
            red0[i, q : q + 1, :] = bias_acc[:, pl.ds((4 * q + i) * 128, 128)]

    def layer_part(q, cols):
        block = weights[0, :, q, :, :, :, cols].reshape(SPAN, BLOCK)
        return jnp.dot(states[:, pl.ds(q * SPAN, SPAN)], block, preferred_element_type=F32)

    def grad_part(q, n):
        lanes = pl.ds(q * SPAN, SPAN)
        rows = None
        for w, value in ((1, gate_g), (2, cand_g)):
            block = weights[w, n, :, :, :, :, lanes].reshape(BLOCK, SPAN)
            term = lax.dot_general(value[:, lanes], block, NT, preferred_element_type=F32)
            rows = term if rows is None else rows + term
        return rows

    def accumulate_layer(q):
        def body(cols, n):
            layer_acc[:, cols] = layer_part(q, cols) + (layer_acc[:, cols] if q else x_p[:, cols].astype(F32))

        blocks(body)

    def accumulate_grad(q):
        def body(cols, n):
            grad_acc[:, cols] = grad_part(q, n) + (grad_acc[:, cols] if q else 0.0)

        blocks(body)

    def poll(q):
        if q == 1:
            for w in range(3):
                for phase in range(2):
                    gather.shared(w, phase, 0)
        if 0 <= q < CHUNKS:
            gather.near(2, q)
            if q + 1 < CHUNKS and q:
                gather.rest(q + 1, (1, 2))
            if q + 2 < CHUNKS:
                gather.rest(q + 2, (-1,))
        if 1 <= q <= CHUNKS:
            gather.far(2, q - 1)

    last = CHUNKS - 1
    poll(0)
    for t in range(CHUNKS + 3):
        if t < CHUNKS:
            poll(t + 1)
            stage_gates(t)
            if t == 0:
                gather_pair()
            forward_scan(t)
            stage_back(t)
            backward_scan(t)
            summarise(t)
        for level in range(3):
            if 0 <= t - 1 - level < CHUNKS:
                compose(level, t - 1 - level)
        if t >= 3:
            settle(t - 3)
            gradients(t - 3)
            if t - 3 < last - 1:
                accumulate_layer(t - 3)
                accumulate_grad(t - 3)

    def reduce_copy(dz, dc):
        k = dz * 2 + dc
        return remote(
            red0.at[lax.rem(z + dz, 4)], red_in.at[k], red_send.at[k], red_recv.at[k], place.column(dz, dc)
        )

    for dz, dc in column_peers:
        reduce_copy(dz, dc).start()
    accumulate_layer(last - 1)
    accumulate_grad(last - 1)

    own_lanes = pl.ds(pl.multiple_of(z * 128, 128), 128)
    turn = lax.rem(128 - 32 * y, 128)
    state_grad_ref[...] = pltpu.roll(vectors[x, 12, :, own_lanes], turn, 1)[:, :32]

    inverse_rows = inverse[...]

    def unit_block(n, row_sum):
        cols = pl.ds(pl.multiple_of(n * BLOCK, BLOCK), BLOCK)
        rows = (grad_part(last, n) + grad_acc[:, cols]) * gain_ref[:, cols]
        grad_acc[:, cols] = rows
        unit = x_p[:, cols].astype(F32) * inverse_rows
        return row_sum + jnp.sum(rows * unit, axis=1, keepdims=True)

    row_sum = lax.fori_loop(0, WIDTH // BLOCK, unit_block, jnp.zeros((TOKENS, 1), F32))
    mean = row_sum * (1.0 / WIDTH)

    for dz, dc in column_peers:
        reduce_copy(dz, dc).wait_recv()
    part = red0[z]
    for dz, dc in column_peers:
        part = part + red_in[dz * 2 + dc]
    for j in range(4):
        red_x[0, j] = part[j : j + 1, :]

    def copy_x(step):
        return remote(
            red_x.at[0, lax.rem(x + step, 4)], red_x.at[step, 0], last_send.at[0, step - 1],
            last_recv.at[0, step - 1], place.line("x", step),
        )

    for step in (1, 2, 3):
        copy_x(step).start()

    def finish_layer(cols, n):
        rows = layer_part(last, cols) + layer_acc[:, cols]
        layer_ref[:, cols] = rows.astype(BF16)

    blocks(finish_layer)

    for step in (1, 2, 3):
        copy_x(step).wait_recv()
    red_y[y] = red_x[0, x] + red_x[1, 0] + red_x[2, 0] + red_x[3, 0]
    last_line = LineExchange(place, "y", lambda v: red_y.at[v], last_send, last_recv, 1)
    last_line.start()

    def finish_grad(cols, n):
        unit = x_p[:, cols].astype(F32) * inverse_rows
        rows = g_p[:, cols].astype(F32) + inverse_rows * (grad_acc[:, cols] - unit * mean)
        grad_ref[:, cols] = rows.astype(BF16)

    blocks(finish_grad)

    for phase in range(3):
        for q in range(CHUNKS if phase == 2 else 1):
            gather.drain(phase, q)
    for line in small_lines + lines[0] + lines[1] + lines[2]:
        line.drain()
    for dz, dc in column_peers:
        reduce_copy(dz, dc).wait_send()
    for step in (1, 2, 3):
        copy_x(step).wait_send()
    last_line.arrive()
    bias_total = red_y[0] + red_y[1] + red_y[2] + red_y[3]
    bias_grad_ref[...] = pltpu.roll(bias_total, turn, 1)[:, :32]
    last_line.drain()


def restore_kernel(layer_ref, grad_ref, small0_ref, small1_ref, layer_out, grad_out, small0_out, small1_out):
    row = lax.broadcasted_iota(jnp.int32, (TOKENS, TOKENS), 0)
    column = lax.broadcasted_iota(jnp.int32, (TOKENS, TOKENS), 1)
    restore = jnp.where(row == lax.rem(column, 8) * STEPS + column // 8, 1.0, 0.0).astype(BF16)
    for source, target in ((layer_ref, layer_out), (grad_ref, grad_out)):
        target[...] = jnp.dot(restore, source[...], preferred_element_type=F32).astype(BF16)
    small0_out[...] = small0_ref[...]
    small1_out[...] = small1_ref[...]


def on_device(inputs, output_grad, norm_gain, gate_bias, state_in, w_gate, w_cand, w_out):
    whole = lambda rows, dtype: pltpu.VMEM((rows, WIDTH), dtype)
    dma = pltpu.SemaphoreType.DMA
    anywhere, vmem = pl.BlockSpec(memory_space=pl.ANY), pl.BlockSpec(memory_space=pltpu.VMEM)
    halves = (2, 16, WIDTH)
    layer, grad, state_grad, bias_grad = pl.pallas_call(
        kernel,
        out_shape=(
            jax.ShapeDtypeStruct((TOKENS, WIDTH), BF16),
            jax.ShapeDtypeStruct((TOKENS, WIDTH), BF16),
            jax.ShapeDtypeStruct((1, 32), F32),
            jax.ShapeDtypeStruct((1, 32), F32),
        ),
        in_specs=[anywhere, anywhere, vmem, vmem, vmem, anywhere, anywhere, anywhere],
        out_specs=[vmem] * 4,
        scratch_shapes=[
            pltpu.VMEM((3, 4, 4, 4, 2, 16, WIDTH), BF16),
            pltpu.VMEM((4, 4, 4, 2, 128), F32),
            whole(2, F32),
            whole(TOKENS, BF16), whole(TOKENS, BF16),
            whole(TOKENS, BF16), whole(TOKENS, BF16), whole(TOKENS, BF16),
            pltpu.VMEM((TOKENS, 1), F32),
            whole(TOKENS, F32), whole(TOKENS, F32), whole(TOKENS, F32), whole(TOKENS, F32), whole(TOKENS, F32),
            whole(TOKENS, BF16), whole(TOKENS, BF16), whole(TOKENS, BF16),
            whole(TOKENS, F32), whole(TOKENS, F32),
            whole(8, F32), whole(8, F32), whole(8, F32), whole(8, F32), whole(8, F32),
            pltpu.VMEM((3, CHUNKS, 4, 4, SPAN), F32),
            pltpu.VMEM((CHUNKS, 13, 1, SPAN), F32),
            whole(1, F32),
            pltpu.VMEM((4, 4, 128), F32),
            pltpu.VMEM((16, 4, 128), F32),
            pltpu.VMEM((4, 4, 1, 128), F32),
            pltpu.VMEM((4, 1, 128), F32),
            dma((3,)), dma((2,)),
            dma((3, 3, 4, CHUNKS)), dma((3, 3, 4, CHUNKS)), dma((3, 3, 4, CHUNKS)), dma((3, 3, 4, CHUNKS)),
            dma((3, 3)), dma((3, 3)), dma((3 * CHUNKS, 3)), dma((3 * CHUNKS, 3)),
            dma((16,)), dma((16,)), dma((2, 3)), dma((2, 3)),
        ],
        compiler_params=pltpu.CompilerParams(
            collective_id=0, has_side_effects=True, vmem_limit_bytes=62 * 1024 * 1024
        ),
        name="mixer",
    )(
        inputs[0], output_grad[0], norm_gain[None], gate_bias[None], state_in,
        w_gate.reshape(halves), w_cand.reshape(halves), w_out.reshape(halves),
    )
    part = pl.BlockSpec((TOKENS, BLOCK), lambda n: (0, n))
    short = pl.BlockSpec((1, 32), lambda n: (0, 0))
    layer, grad, state_grad, bias_grad = pl.pallas_call(
        restore_kernel,
        out_shape=(
            jax.ShapeDtypeStruct((TOKENS, WIDTH), BF16),
            jax.ShapeDtypeStruct((TOKENS, WIDTH), BF16),
            jax.ShapeDtypeStruct((1, 32), F32),
            jax.ShapeDtypeStruct((1, 32), F32),
        ),
        grid=(WIDTH // BLOCK,),
        in_specs=[part, part, short, short],
        out_specs=[part, part, short, short],
        name="restore",
    )(layer, grad, state_grad, bias_grad)
    return (layer[None], grad[None], state_grad, bias_grad[0])


def solution(mesh):
    return jax.shard_map(
        on_device,
        mesh=mesh,
        in_specs=(
            P("batch", "seq", None),
            P("batch", "seq", None),
            P(),
            P("seq"),
            P("batch", "seq"),
            P("seq", None),
            P("seq", None),
            P("seq", None),
        ),
        out_specs=(P("batch", "seq", None), P("batch", "seq", None), P("batch", "seq"), P("seq")),
        check_vma=False,
    )
```

time: 117 us -> 106 us (0.906)
  local copies, waits for them, and re-layouts: 5.93 us -> 0 us
  Pallas kernels: 110 us -> 105 us
    pallas_call x1, Pallas kernels: 110 us -> 101 us  [on_device(): pl.pallas_call(kernel, out_shape=(jax.ShapeDtypeStruct((TOKENS, WIDTH), B...]
    unnamed x14 -> x0, local copies, waits for them, and re-layouts: 5.76 us -> none
    pallas_call x0 -> x1, Pallas kernels: none -> 4.18 us  [on_device(): pl.pallas_call(restore_kernel, out_shape=(jax.ShapeDtypeStruct((TOKENS, W...]
where the time goes in v3:
time: 106 us
  Pallas kernels  105 us (99%)
    pallas_call x1, Pallas kernels, on_device(): pl.pallas_call(kernel, out_shape=(jax.ShapeDtypeStruct((TOKENS, WIDTH), B...  101 us
    pallas_call x1, Pallas kernels, on_device(): pl.pallas_call(restore_kernel, out_shape=(jax.ShapeDtypeStruct((TOKENS, W...  4.18 us

profile of v3, /device:TPU:1, one launch (start us, length us, event | category | flops | bytes accessed | tf_op | source)
XLA Modules:
  0.0 105.7 jit_solution(12132299710490915958)
XLA Ops:
  0.6 100.9 %mixer.1 = (bf16[256,2048]{1,0:T(8,128)(2,1)}, bf16[256,2048]{1,0:T(8,128)(2,1)}, f32[1,32]{1,0:T(1,128)}, f32[1,32]{1,0:T(1,128)}) custom-call(bf16[256,2048]{1,0:T(8,128)(2,1)} %bitcast.10, bf16[256,2048]{1,0:T(8,128)(2,1)} %bitcast.11, f32[1,2048]{1,0:T(1,128)} %bitcast.15, f32[1,32]{1,0:T(1,128)} %bitcast.16, f32[1,32]{1,0:T(1,128)} %state_ref.1, ...), custom_call_target="tpu_custom_call" | custom-call | tf_op jit(solution)/shard_map/mixer/pallas_call | solution.py:582
  101.6 4.2 %restore.1 = (bf16[256,2048]{1,0:T(8,128)(2,1)}, bf16[256,2048]{1,0:T(8,128)(2,1)}, f32[1,32]{1,0:T(1,128)}, f32[1,32]{1,0:T(1,128)}) custom-call(bf16[256,2048]{1,0:T(8,128)(2,1)} %get-tuple-element.12.layer_ref, bf16[256,2048]{1,0:T(8,128)(2,1)} %get-tuple-element.13.grad_ref, f32[1,32]{1,0:T(1,128)} %get-tuple-element.14.small0_ref, ...), custom_call_target="tpu_custom_call" | custom-call | tf_op jit(solution)/shard_map/restore/pallas_call | solution.py:625
